TPU v7x, 32 devices: a whole 2x2x4 slice. The times are simulated.
32 devices in a mesh: blk: 4 (over y, x), dp: 8 (over z, core).
Axes of the slice: x: 2, y: 2, z: 4, core: 2. Of those that a mesh axis runs over, the one named last changes fastest.
Arguments:
- item_ids: int32 [8, 2048], P('dp', 'blk'), may hold values from 0 to 2047
- pos_buckets: int32 [8, 2048], P('dp', 'blk'), may hold values from 0 to 63
- time_buckets: int32 [8, 2048], P('dp', 'blk'), may hold values from 0 to 63
- item_table: bfloat16 [2048, 512], P('dp'), may hold values from -6 to 6
- proj_in: float32 [512, 2048], P(('blk', 'dp')), may hold values from -0.25 to 0.25
- proj_out: float32 [512, 512], P(('blk', 'dp')), may hold values from -0.375 to 0.375
- small_params: float32 [6, 512], P(None, ('blk', 'dp')), may hold values from -4 to 4, as said below
- out_grad: bfloat16 [8, 2048, 512], P('dp', 'blk'), may hold values from -6 to 6
- moment_in: float32 [512, 2048], P(('blk', 'dp')), may hold values from -384 to 384
- second_in: float32 [512, 2048], P(('blk', 'dp')), may hold values from 4096 to 16384
- moment_out: float32 [512, 512], P(('blk', 'dp')), may hold values from -384 to 384
- second_out: float32 [512, 512], P(('blk', 'dp')), may hold values from 4096 to 16384
- moment_small: float32 [6, 512], P(None, ('blk', 'dp')), may hold values from -384 to 384
- second_small: float32 [6, 512], P(None, ('blk', 'dp')), may hold values from 4096 to 16384
Outputs:
- layer_out: bfloat16 [8, 2048, 512], P('dp', 'blk')
- input_grad: float32 [8, 2048, 512], P('dp', 'blk')
- table_grad: float32 [2048, 512], P(('blk', 'dp'))
- item_counts: float32 [2048], P(('blk', 'dp'))
- log_q: float32 [2048], P(('blk', 'dp'))
- new_moment_in: float32 [512, 2048], P(('blk', 'dp'))
- new_second_in: float32 [512, 2048], P(('blk', 'dp'))
- new_proj_in: float32 [512, 2048], P(('blk', 'dp'))
- new_moment_out: float32 [512, 512], P(('blk', 'dp'))
- new_second_out: float32 [512, 512], P(('blk', 'dp'))
- new_proj_out: float32 [512, 512], P(('blk', 'dp'))
- new_moment_small: float32 [6, 512], P(None, ('blk', 'dp'))
- new_second_small: float32 [6, 512], P(None, ('blk', 'dp'))
- new_small: float32 [6, 512], P(None, ('blk', 'dp'))
Inputs may be any that keep to these rules, and one draw needn't show every extreme that they name: `small_params`: rows 0 and 2 lie near one, rows 1 and 3 near zero, rows 4 and 5 of order one.
All inputs are finite; a program needn't handle non-finite values.
Results may differ from a plain program's by a relative error of at most 0.012.
Values may be sent and summed in bfloat16 or wider, within the bound.
A program may use at most 128 MiB of HBM per device.

v0:
```python
import math

import jax
import jax.numpy as jnp
from jax import lax
from jax.sharding import PartitionSpec as P

D = 512
H = 8
HEAD = 64
NB = 64


norm_eps = 1e-05
beta_first = 0.5
beta_second = 0.5
adam_eps = 1e-08
weight_decay = 0.01
rate_in = 0.05
rate_out = 0.06
rate_small = 0.3
step_number = 3


def standardize(values):
    centered = values - jnp.mean(values, axis=-1, keepdims=True)
    inverse = lax.rsqrt(jnp.mean(centered * centered, axis=-1, keepdims=True) + norm_eps)
    return (centered * inverse, inverse)


def norm_back(grad_hat, normal_hat, inverse):
    mean_grad = jnp.mean(grad_hat, axis=-1, keepdims=True)
    mean_cross = jnp.mean(grad_hat * normal_hat, axis=-1, keepdims=True)
    return (grad_hat - mean_grad - normal_hat * mean_cross) * inverse


def silu_slope(values):
    logistic = jax.nn.sigmoid(values)
    return logistic * (1.0 + values * (1.0 - logistic))


def adam_update(weight, grad, moment, second, rate):
    new_moment = beta_first * moment + (1.0 - beta_first) * grad
    new_second = beta_second * second + (1.0 - beta_second) * grad * grad
    moment_hat = new_moment / (1.0 - beta_first**step_number)
    second_hat = new_second / (1.0 - beta_second**step_number)
    new_weight = weight - rate * (
        moment_hat / (jnp.sqrt(second_hat) + adam_eps) + weight_decay * weight
    )
    return (new_moment, new_second, new_weight)


def per_device(
    item_ids,
    pos_buckets,
    time_buckets,
    item_table,
    proj_in,
    proj_out,
    small_params,
    out_grad,
    moment_in,
    second_in,
    moment_out,
    second_out,
    moment_small,
    second_small,
):
    seq_count, group = item_ids.shape
    length = group * lax.axis_size("blk")
    devices = lax.axis_size("blk") * lax.axis_size("dp")
    items = item_table.shape[0] * lax.axis_size("dp")
    tokens = seq_count * group
    scale = HEAD ** (-0.5)
    copy_in, copy_out, copy_small = (
        lax.all_gather(proj_in.astype(jnp.bfloat16), ("blk", "dp"), axis=0, tiled=True),
        lax.all_gather(proj_out.astype(jnp.bfloat16), ("blk", "dp"), axis=0, tiled=True),
        lax.all_gather(small_params.astype(jnp.bfloat16), ("blk", "dp"), axis=1, tiled=True),
    )
    small_float = copy_small.astype(jnp.float32)
    flat_ids = item_ids.reshape(tokens)
    portion = lax.all_gather(item_table, "dp", axis=0, tiled=True)
    hot = (flat_ids[:, None] == jnp.arange(portion.shape[0], dtype=jnp.int32)[None, :]).astype(
        jnp.bfloat16
    )
    embedded = jnp.dot(hot, portion, preferred_element_type=jnp.float32)
    hat_one, inverse_one = standardize(embedded)
    normed = (hat_one * small_float[0] + small_float[1]).astype(jnp.bfloat16)
    projected = jnp.dot(normed, copy_in, preferred_element_type=jnp.float32)
    activated = jax.nn.silu(projected)
    gate_u = activated[:, :D]
    rounded = activated[:, D:].astype(jnp.bfloat16)
    values = rounded[:, :D].reshape(seq_count, group, H, HEAD)
    queries = rounded[:, D : 2 * D].reshape(seq_count, group, H, HEAD)
    keys_own = rounded[:, 2 * D :].reshape(seq_count, group, H, HEAD)
    pos_table = small_float[4].reshape(H, NB)
    time_table = small_float[5].reshape(H, NB)
    buckets = jnp.arange(NB, dtype=jnp.int32)
    time_hot = (time_buckets[:, :, None] == buckets).astype(jnp.float32)
    query_bias = jnp.einsum("scb,hb->shc", time_hot, time_table)
    query_first = lax.axis_index("blk") * group
    query_pos = query_first + jnp.arange(group, dtype=jnp.int32)
    query_last = query_first + group - 1
    pos_sent = pos_buckets.astype(jnp.bfloat16)

    def tile_scores(key_blk, bucket_blk, key_start):
        pos_hot = (bucket_blk.astype(jnp.int32)[:, :, None] == buckets).astype(jnp.float32)
        key_bias = jnp.einsum("sjb,hb->shj", pos_hot, pos_table)
        raw_scores = (
            jnp.einsum("sihd,sjhd->shij", queries, key_blk, preferred_element_type=jnp.float32)
            * scale
        )
        raw_scores = raw_scores + query_bias[:, :, :, None] + key_bias[:, :, None, :]
        key_pos = key_start + jnp.arange(key_blk.shape[1], dtype=jnp.int32)
        allowed = (query_pos[:, None] >= key_pos[None, :])[None, None]
        return (raw_scores, allowed, pos_hot)

    attend_init = jnp.zeros((seq_count, group, H, HEAD), jnp.float32)
    running = attend_init
    key_part = lax.all_gather(keys_own, "blk", axis=1, tiled=True)
    value_part = lax.all_gather(values, "blk", axis=1, tiled=True)
    bucket_part = lax.all_gather(pos_sent, "blk", axis=1, tiled=True)
    span = key_part.shape[1]
    rows_blk = math.gcd(span, 512)

    def fold_step(carried, block_idx):
        key_start = block_idx * rows_blk
        key_blk = lax.dynamic_slice_in_dim(key_part, key_start, rows_blk, 1)
        value_blk = lax.dynamic_slice_in_dim(value_part, key_start, rows_blk, 1)
        bucket_blk = lax.dynamic_slice_in_dim(bucket_part, key_start, rows_blk, 1)

        def fold_compute(current):
            raw_scores, allowed, pos_hot = tile_scores(key_blk, bucket_blk, key_start)
            weights = jnp.where(allowed, jax.nn.silu(raw_scores) / length, 0.0).astype(jnp.bfloat16)
            return current + jnp.einsum(
                "shij,sjhd->sihd", weights, value_blk, preferred_element_type=jnp.float32
            )

        return (
            lax.cond(key_start <= query_last, fold_compute, lambda current: current, carried),
            None,
        )

    running, _ = lax.scan(fold_step, running, jnp.arange(span // rows_blk, dtype=jnp.int32))
    attended = running
    attended = attended.reshape(tokens, D)
    hat_two, inverse_two = standardize(attended)
    normed_two = hat_two * small_float[2] + small_float[3]
    gated = (normed_two * gate_u).astype(jnp.bfloat16)
    result = embedded + jnp.dot(gated, copy_out, preferred_element_type=jnp.float32)
    layer_out = result.astype(jnp.bfloat16).reshape(seq_count, group, D)
    cotangent = out_grad.reshape(tokens, D)
    grad_out_weight = jnp.einsum("td,te->de", gated, cotangent, preferred_element_type=jnp.float32)
    grad_gated = jnp.einsum("te,de->td", cotangent, copy_out, preferred_element_type=jnp.float32)
    grad_u = grad_gated * normed_two
    grad_norm_two = grad_gated * gate_u
    grad_gain_two = jnp.sum(grad_norm_two * hat_two, axis=0)
    grad_shift_two = jnp.sum(grad_norm_two, axis=0)
    grad_attended = norm_back(grad_norm_two * small_float[2], hat_two, inverse_two).astype(
        jnp.bfloat16
    )
    grad_attended = grad_attended.reshape(seq_count, group, H, HEAD)
    key_whole, value_whole, bucket_whole = (
        lax.all_gather(keys_own, "blk", axis=1, tiled=True),
        lax.all_gather(values, "blk", axis=1, tiled=True),
        lax.all_gather(pos_sent, "blk", axis=1, tiled=True),
    )
    rows_back = math.gcd(length, 512)

    def back_step(carried, block_idx):
        grad_query, grad_pos, grad_qbias = carried
        key_start = block_idx * rows_back
        key_blk = lax.dynamic_slice_in_dim(key_whole, key_start, rows_back, 1)
        value_blk = lax.dynamic_slice_in_dim(value_whole, key_start, rows_back, 1)
        bucket_blk = lax.dynamic_slice_in_dim(bucket_whole, key_start, rows_back, 1)

        def back_compute(operand):
            raw_scores, allowed, pos_hot = tile_scores(key_blk, bucket_blk, key_start)
            grad_weights = jnp.einsum(
                "sihd,sjhd->shij", grad_attended, value_blk, preferred_element_type=jnp.float32
            )
            grad_raw = jnp.where(
                allowed, grad_weights / length * silu_slope(raw_scores), 0.0
            ).astype(jnp.bfloat16)
            grad_raw_float = grad_raw.astype(jnp.float32)
            part_query = (
                jnp.einsum("shij,sjhd->sihd", grad_raw, key_blk, preferred_element_type=jnp.float32)
                * scale
            )
            part_pos = jnp.einsum("shj,sjb->hb", jnp.sum(grad_raw_float, axis=2), pos_hot)
            part_qbias = jnp.sum(grad_raw_float, axis=3)
            weights = jnp.where(allowed, jax.nn.silu(raw_scores) / length, 0.0).astype(jnp.bfloat16)
            part_key = (
                jnp.einsum("shij,sihd->sjhd", grad_raw, queries, preferred_element_type=jnp.float32)
                * scale
            )
            part_value = jnp.einsum(
                "shij,sihd->sjhd", weights, grad_attended, preferred_element_type=jnp.float32
            )
            paired = jnp.concatenate(
                [
                    part_key.reshape(seq_count, rows_back, D),
                    part_value.reshape(seq_count, rows_back, D),
                ],
                axis=-1,
            )
            return (part_query, part_pos, part_qbias, paired)

        def skip_tile(operand):
            empty = (
                jnp.zeros((seq_count, group, H, HEAD), jnp.float32),
                jnp.zeros((H, NB), jnp.float32),
                jnp.zeros((seq_count, H, group), jnp.float32),
            )
            return empty + (jnp.zeros((seq_count, rows_back, 2 * D), jnp.float32),)

        parts = lax.cond(key_start <= query_last, back_compute, skip_tile, 0)
        summed = (grad_query + parts[0], grad_pos + parts[1], grad_qbias + parts[2])
        return (summed, parts[3])

    back_init = (
        jnp.zeros((seq_count, group, H, HEAD), jnp.float32),
        jnp.zeros((H, NB), jnp.float32),
        jnp.zeros((seq_count, H, group), jnp.float32),
    )
    (grad_query, grad_pos_table, grad_qbias), stacked = lax.scan(
        back_step, back_init, jnp.arange(length // rows_back, dtype=jnp.int32)
    )
    kv_terms = stacked.transpose(1, 0, 2, 3).reshape(seq_count, length, 2 * D)
    kv_own = lax.psum_scatter(kv_terms, "blk", scatter_dimension=1, tiled=True)
    grad_key = kv_own[:, :, :D].reshape(tokens, D)
    grad_value = kv_own[:, :, D:].reshape(tokens, D)
    grad_time_table = jnp.einsum("shc,scb->hb", grad_qbias, time_hot)
    grad_acts = jnp.concatenate(
        [grad_u, grad_value, grad_query.reshape(tokens, D), grad_key], axis=-1
    )
    grad_pre = (grad_acts * silu_slope(projected)).astype(jnp.bfloat16)
    grad_in_weight = jnp.einsum("td,tf->df", normed, grad_pre, preferred_element_type=jnp.float32)
    grad_normed = jnp.einsum("tf,df->td", grad_pre, copy_in, preferred_element_type=jnp.float32)
    grad_gain_one = jnp.sum(grad_normed * hat_one, axis=0)
    grad_shift_one = jnp.sum(grad_normed, axis=0)
    grad_embed = cotangent.astype(jnp.float32) + norm_back(
        grad_normed * small_float[0], hat_one, inverse_one
    )
    input_grad = grad_embed.reshape(seq_count, group, D)
    grad_small = jnp.stack(
        [
            grad_gain_one,
            grad_shift_one,
            grad_gain_two,
            grad_shift_two,
            grad_pos_table.reshape(D),
            grad_time_table.reshape(D),
        ]
    )
    counts_local = jnp.sum(
        (flat_ids[:, None] == jnp.arange(items, dtype=jnp.int32)[None, :]).astype(jnp.float32),
        axis=0,
    )
    shard_in, shard_out, shard_small, item_counts = (
        lax.psum_scatter(grad_in_weight, ("blk", "dp"), scatter_dimension=0, tiled=True),
        lax.psum_scatter(grad_out_weight, ("blk", "dp"), scatter_dimension=0, tiled=True),
        lax.psum_scatter(grad_small, ("blk", "dp"), scatter_dimension=1, tiled=True),
        lax.psum_scatter(counts_local, ("blk", "dp"), scatter_dimension=0, tiled=True),
    )
    grad_rounded = grad_embed.astype(jnp.bfloat16)
    hot = (
        flat_ids[:, None]
        == jnp.arange(items // devices * lax.axis_size(("blk", "dp")), dtype=jnp.int32)[None, :]
    ).astype(jnp.bfloat16)
    table_grad = lax.psum_scatter(
        jnp.einsum("tr,td->rd", hot, grad_rounded, preferred_element_type=jnp.float32),
        ("blk", "dp"),
        scatter_dimension=0,
        tiled=True,
    )
    log_q = jnp.log(jnp.maximum(item_counts, 1.0) / (seq_count * lax.axis_size("dp") * length))
    new_moment_in, new_second_in, new_proj_in = adam_update(
        proj_in, shard_in, moment_in, second_in, rate_in
    )
    new_moment_out, new_second_out, new_proj_out = adam_update(
        proj_out, shard_out, moment_out, second_out, rate_out
    )
    new_moment_small, new_second_small, new_small = adam_update(
        small_params, shard_small, moment_small, second_small, rate_small
    )
    return (
        layer_out,
        input_grad,
        table_grad,
        item_counts,
        log_q,
        new_moment_in,
        new_second_in,
        new_proj_in,
        new_moment_out,
        new_second_out,
        new_proj_out,
        new_moment_small,
        new_second_small,
        new_small,
    )


def solution(mesh):
    placed = (
        P("dp", "blk"),
        P("dp", "blk"),
        P("dp", "blk"),
        P("dp", None),
        P(("blk", "dp"), None),
        P(("blk", "dp"), None),
        P(None, ("blk", "dp")),
        P("dp", "blk", None),
        P(("blk", "dp"), None),
        P(("blk", "dp"), None),
        P(("blk", "dp"), None),
        P(("blk", "dp"), None),
        P(None, ("blk", "dp")),
        P(None, ("blk", "dp")),
    )
    return jax.shard_map(
        per_device,
        mesh=mesh,
        in_specs=placed,
        out_specs=(
            P("dp", "blk", None),
            P("dp", "blk", None),
            P(("blk", "dp"), None),
            P(("blk", "dp")),
            P(("blk", "dp")),
            P(("blk", "dp"), None),
            P(("blk", "dp"), None),
            P(("blk", "dp"), None),
            P(("blk", "dp"), None),
            P(("blk", "dp"), None),
            P(("blk", "dp"), None),
            P(None, ("blk", "dp")),
            P(None, ("blk", "dp")),
            P(None, ("blk", "dp")),
        ),
        check_vma=False,
    )
```

profile of v0, /device:TPU:0, one launch (start us, length us, event | category | flops | bytes accessed | tf_op | source)
XLA Modules:
  0.0 969.7 jit_solution(2810416468792286087)
XLA Ops:
  8.0 1.5 convert_element_type.90
  10.3 43.8 %all-gather = bf16[32,16,6]{1,2,0:T(8,128)(2,1)S(1)} all-gather(bf16[1,16,6]{1,2,0:T(8,128)(2,1)S(1)} %convert_bitcast_fusion), channel_id=1, replica_groups=mesh['blk'=4,'dp'=8] {'blk','dp'}, dimensions={0}, use_global_device_ids=true | all-gather | bytes 6336 | tf_op jit(solution)/shard_map/all_gather | solution.py:78
  54.3 3.1 fusion.117
  57.6 43.8 %all-gather.8.cloned.1.call-done = bf16[512,2048]{1,0:T(8,128)(2,1)} async-done(((bf16[16,2048]{1,0:T(8,128)(2,1)}), bf16[512,2048]{1,0:T(8,128)(2,1)}) %all-gather.8.cloned.1.call-update) | async-done | bytes 2097168 | tf_op jit(solution)/shard_map/all_gather | solution.py:76
  101.4 6.8 fusion.113
  110.8 8.0 all_gather.29
  119.0 42.0 %all_gather.30 = bf16[512,512]{1,0:T(8,128)(2,1)S(1)} all-gather(bf16[16,512]{1,0:T(8,128)(2,1)S(1)} %convert_element_type.93), channel_id=1, replica_groups=mesh['blk'=4,'dp'=8] {'blk','dp'}, dimensions={0}, use_global_device_ids=true | all-gather | bytes 540672 | tf_op jit(solution)/shard_map/all_gather | solution.py:77
  161.2 21.0 %all-gather.10.cloned.1.call-done = bf16[1,2048,8,64]{1,3,2,0:T(8,128)(2,1)} async-done(((bf16[1,512,8,64]{1,3,2,0:T(8,128)(2,1)}), bf16[1,2048,8,64]{1,3,2,0:T(8,128)(2,1)}) %all-gather.10.cloned.1.call-update) | async-done | bytes 2097168 | tf_op jit(solution)/shard_map/all_gather | solution.py:121
  182.4 11.4 %while.31 = (s32[]{:T(128)}, f32[1,512,8,64]{1,3,2,0:T(8,128)S(1)}, s32[4]{0:T(128)S(1)}, s32[]{:T(128)}, bf16[1,2048,8,64]{1,3,2,0:T(8,128)(2,1)}, /*index=5*/b...) while((s32[]{:T(128)}, f32[1,512,8,64]{1,3,2,0:T(8,128)S(1)}, ...), condition=%wide.region_5.6_spmd.clone, body=%wide.region_2.5_spmd.clone.sunk | while | flops 558925312 | bytes 4263737 | solution.py:144
  183.7 6.2 conditional.6
  184.3 5.6 fusion.21
  194.5 3.9 multiply_reduce_fusion
  199.8 53.5 %while.32 = (s32[]{:T(128)}, f32[1,512,8,64]{1,3,2,0:T(8,128)}, f32[8,64]{1,0:T(8,128)S(1)}, f32[1,8,512]{2,1,0:T(8,128)S(1)}, f32[4,1,512,1024]{3,2,0,1:T(8,128...) while((s32[]{:T(128)}, f32[1,512,8,64]{1,3,2,0:T(8,128)}, ...), condition=%wide.region_15.16_spmd.clone, body=%wide.region_10.0_spmd.clone.sunk | while | flops 1401752064 | bytes 67564776 | solution.py:226
  201.2 17.8 %conditional.7 = (f32[1,512,8,64]{1,3,2,0:T(8,128)S(1)}, f32[8,64]{1,0:T(8,128)S(1)}, f32[1,8,512]{2,1,0:T(8,128)S(1)}, f32[1,1,512,1024]{2,3,1,0:T(8,128)S(1)}) conditional(s32[]{:T(128)} %convert_element_type.138, () %tuple.118, (s32[]{:T(128)}, bf16[1,2048,8,64]{1,3,2,0:T(8,128)(2,1)}, s32[]{:T(128)}, bf16[1,2048,8,64]{1,3,2,0:T(8,128)(2,1)}, ...), branch_computations={%region_11.11_spmd, %region_12.14_spmd} | conditional | flops 1401218560 | bytes 51778168 | solution.py:217
  201.8 3.4 fusion.56
  205.2 3.2 fusion.52
  208.4 6.7 convert_reduce_fusion
  215.1 2.0 fusion.54
  217.4 1.4 convolution_multiply_fusion
  220.2 1.8 copy.136
  222.0 3.2 constant_dynamic-update-slice_fusion.2
  227.1 2.5 select_add_fusion.6
  229.5 1.8 copy.136
  231.4 3.2 constant_dynamic-update-slice_fusion.2
  236.4 2.5 select_add_fusion.6
  238.9 1.8 copy.136
  240.7 3.2 constant_dynamic-update-slice_fusion.2
  245.7 2.5 select_add_fusion.6
  248.2 1.8 copy.136
  250.0 3.2 constant_dynamic-update-slice_fusion.2
  254.5 1.4 fusion.91
  256.6 153.7 %reduce-scatter.8.cloned.1.call-done = f32[1,512,1024]{2,1,0:T(8,128)} async-done(((f32[1,2048,1024]{2,1,0:T(8,128)}), f32[1,512,1024]{2,1,0:T(8,128)}) %reduce-scatter.8.cloned.1.call-update) | async-done | bytes 2097168 | tf_op jit(solution)/shard_map/reduce_scatter | solution.py:230
  410.3 1.9 slice_bitcast_fusion.1
  413.1 2.7 fusion.80
  415.9 2.3 fusion.118
  418.2 1.6 copy.108
  421.3 4.9 fusion.106
  427.3 4.7 fusion.84
  432.5 39.4 %all-reduce = f32[2048]{0:T(1024)S(1)} all-reduce(f32[2048]{0:T(1024)S(1)} %convert_reduce_fusion.2), channel_id=4, replica_groups=mesh['blk'=4,'dp'=8] {'blk','dp'}, use_global_device_ids=true, to_apply=%region_21.22.clone | all-reduce | flops 2048 | bytes 16384
  473.8 2.1 copy.110
  475.9 71.5 %reduce-scatter.14.cloned.1.call-done = f32[16,512]{1,0:T(8,128)} async-done(((f32[512,512]{1,0:T(8,128)}), f32[16,512]{1,0:T(8,128)}) %reduce-scatter.14.cloned.1.call-update) | async-done | bytes 32784 | tf_op jit(solution)/shard_map/reduce_scatter | solution.py:262
  547.5 1.5 multiply_subtract_fusion.1
  548.9 1.4 fusion.108
  551.6 128.0 %reduce-scatter.16.cloned.1.call-done = f32[16,6]{1,0:T(8,128)} async-done(((f32[512,6]{1,0:T(8,128)}), f32[16,6]{1,0:T(8,128)}) %reduce-scatter.16.cloned.1.call-update) | async-done | bytes 400
  680.4 1.3 multiply_subtract_fusion.2
  681.7 138.9 %reduce-scatter.12.cloned.1.call-done = f32[16,2048]{1,0:T(8,128)} async-done(((f32[512,2048]{1,0:T(8,128)}), f32[16,2048]{1,0:T(8,128)}) %reduce-scatter.12.cloned.1.call-update) | async-done | bytes 131088 | tf_op jit(solution)/shard_map/reduce_scatter | solution.py:261
  820.6 1.7 multiply_subtract_fusion
  822.3 140.9 %reduce-scatter.10.cloned.1.call-done = f32[64,512]{1,0:T(8,128)} async-done(((f32[2048,512]{1,0:T(8,128)}), f32[64,512]{1,0:T(8,128)}) %reduce-scatter.10.cloned.1.call-update) | async-done | bytes 131088 | tf_op jit(solution)/shard_map/reduce_scatter | solution.py:271
  (209 shorter events, 27.1 us)
Async XLA Ops:
  7.2 47.1 %all-gather.6.cloned.1.call-start = ((), (), s32[]{:S(2)}) async-start(), calls=%async_computation.5 | async-start | bytes 2359296 | tf_op jit(solution)/shard_map/all_gather | solution.py:82
  7.9 93.5 %all-gather.8.cloned.1.call-start = ((), (), s32[]{:S(2)}) async-start(), calls=%async_computation.6 | async-start | bytes 2162688 | tf_op jit(solution)/shard_map/all_gather | solution.py:76
  9.5 151.7 %all-gather.12.cloned.1.call-start = ((), (), s32[]{:S(2)}) async-start(), calls=%async_computation.8 | async-start | bytes 2621440 | tf_op jit(solution)/shard_map/all_gather | solution.py:120
  54.2 47.2 %copy-start.16 = (f32[1,512]{1,0:T(1,128)}, f32[1,512]{1,0:T(1,128)S(1)}, u32[]{:S(2)}) copy-start(f32[1,512]{1,0:T(1,128)S(1)} %get-tuple-element.681) | copy-start | bytes 6148
  54.3 47.2 %copy-start.22 = (f32[1,512]{1,0:T(1,128)}, f32[1,512]{1,0:T(1,128)S(1)}, u32[]{:S(2)}) copy-start(f32[1,512]{1,0:T(1,128)S(1)} %get-tuple-element.680) | copy-start | bytes 6148
  57.4 50.8 %copy-start.3 = (f32[512,512]{0,1:T(8,128)}, f32[512,512]{0,1:T(8,128)S(1)}, u32[]{:S(2)}) copy-start(f32[512,512]{0,1:T(8,128)S(1)} %get-tuple-element.683) | copy-start | bytes 3145732
  57.4 50.8 %copy-start.18 = (f32[512]{0:T(512)}, f32[512]{0:T(512)S(1)}, u32[]{:S(2)}) copy-start(f32[512]{0:T(512)S(1)} %broadcast_multiply_fusion.5) | copy-start | bytes 6148
  57.6 50.6 %copy-start.20 = (f32[512]{0:T(512)}, f32[512]{0:T(512)S(1)}, u32[]{:S(2)}) copy-start(f32[512]{0:T(512)S(1)} %add_rsqrt_fusion.1) | copy-start | bytes 6148
  108.2 2.4 copy-start.29
  108.2 2.4 copy-start.15
  108.2 10.6 %copy-start.31 = (s32[1,512]{1,0:T(1,128)S(1)}, s32[1,512]{1,0:T(1,128)}, u32[]{:S(2)}) copy-start(s32[1,512]{1,0:T(1,128)} %param.24) | copy-start | bytes 6148
  109.4 72.9 %all-gather.10.cloned.1.call-start = ((), (), s32[]{:S(2)}) async-start(), calls=%async_computation.7 | async-start | bytes 2621440 | tf_op jit(solution)/shard_map/all_gather | solution.py:121
  110.5 299.8 %reduce-scatter.8.cloned.1.call-start = ((), (), s32[]{:S(2)}) async-start(), calls=%async_computation.9 | async-start | bytes 10485760 | tf_op jit(solution)/shard_map/reduce_scatter | solution.py:230
  161.0 33.5 %copy-start.6 = (bf16[512,512]{1,0:T(8,128)(2,1)}, bf16[512,512]{1,0:T(8,128)(2,1)S(1)}, u32[]{:S(2)}) copy-start(bf16[512,512]{1,0:T(8,128)(2,1)S(1)} %all_gather.30) | copy-start | bytes 1572868
  199.8 1.4 copy-start
  201.8 3.4 copy-start.12
  222.0 3.2 copy-start.1
  225.3 1.4 copy-start
  231.4 3.2 copy-start.1
  234.6 1.4 copy-start
  240.7 3.2 copy-start.1
  243.9 1.4 copy-start
  250.0 3.2 copy-start.1
  253.3 1.2 copy-start.9
  253.3 2.7 copy-start.2
  253.3 3.1 copy-start.32
  253.3 294.2 %reduce-scatter.14.cloned.1.call-start = ((), (), s32[]{:S(2)}) async-start(), calls=%async_computation.12 | async-start | bytes 1081344 | tf_op jit(solution)/shard_map/reduce_scatter | solution.py:262
  255.9 423.7 %reduce-scatter.16.cloned.1.call-start = ((), (), s32[]{:S(2)}) async-start(), calls=%async_computation.13 | async-start | bytes 270336
  410.3 2.8 copy-start.10
  413.1 2.7 copy-start.30
  415.9 2.3 copy-start.5
  415.9 3.9 copy-start.4
  415.9 3.9 copy-start.17
  415.9 3.9 copy-start.19
  415.9 3.9 copy-start.21
  418.2 2.0 copy-start.25
  418.2 2.0 copy-start.26
  418.2 3.1 copy-start.23
  421.2 399.4 %reduce-scatter.12.cloned.1.call-start = ((), (), s32[]{:S(2)}) async-start(), calls=%async_computation.11 | async-start | bytes 4325376 | tf_op jit(solution)/shard_map/reduce_scatter | solution.py:261
  426.1 1.1 copy-start.33
  426.1 537.1 %reduce-scatter.10.cloned.1.call-start = ((), (), s32[]{:S(2)}) async-start(), calls=%async_computation.10 | async-start | bytes 4325376 | tf_op jit(solution)/shard_map/reduce_scatter | solution.py:271
  427.2 4.7 copy-start.27
  427.2 4.7 copy-start.28
  431.9 40.6 %copy-start.7 = (bf16[512,512]{1,0:T(8,128)(2,1)S(1)}, bf16[512,512]{1,0:T(8,128)(2,1)}, u32[]{:S(2)}) copy-start(bf16[512,512]{1,0:T(8,128)(2,1)} %copy-done.6) | copy-start | bytes 1572868
  472.6 207.8 %copy-start.24 = (f32[6,16]{1,0:T(8,128)S(1)}, f32[6,16]{1,0:T(8,128)}, u32[]{:S(2)}) copy-start(f32[6,16]{1,0:T(8,128)} %param.28) | copy-start | bytes 1156
  473.8 346.8 %copy-start.11 = (f32[16,2048]{1,0:T(8,128)S(1)}, f32[16,2048]{1,0:T(8,128)}, u32[]{:S(2)}) copy-start(f32[16,2048]{1,0:T(8,128)} %param.26) | copy-start | bytes 393220
  473.8 346.8 %copy-start.13 = (f32[16,2048]{1,0:T(8,128)S(1)}, f32[16,2048]{1,0:T(8,128)}, u32[]{:S(2)}) copy-start(f32[16,2048]{1,0:T(8,128)} %param.31) | copy-start | bytes 393220
  473.8 346.8 %copy-start.14 = (f32[16,2048]{1,0:T(8,128)S(1)}, f32[16,2048]{1,0:T(8,128)}, u32[]{:S(2)}) copy-start(f32[16,2048]{1,0:T(8,128)} %param.30) | copy-start | bytes 393220
  (1 other events, 1.0 us)
Sparse Core Ops, SparseCore 0:
  9.6 32.2 all-gather.5
  45.4 55.9 all-gather.7
  109.5 35.0 all-gather.11
  146.9 35.3 all-gather.9
  253.4 156.8 reduce-scatter.7
  412.5 134.9 reduce-scatter.13
  549.7 129.8 reduce-scatter.15
  682.0 138.5 reduce-scatter.11
  823.6 139.6 reduce-scatter.9
where the time goes:
time: 971 us; the launch traced here: 970 us
  waiting for transfers between devices  699 us (72%)
  blocking collectives  133 us (14%)
  matrix products  51.7 us (5%)
  local copies, waits for them, and re-layouts  42.9 us (4%)
  other arithmetic  22.7 us (2%)
  between operations  14.3 us (1%)
    reduce_scatter x1, waiting for transfers between devices, per_device(): kv_own = lax.psum_scatter(kv_terms, 'blk', scatter_dimension=1, tiled=True)  154 us
    reduce_scatter x1, waiting for transfers between devices, per_device(): lax.psum_scatter(jnp.einsum('tr,td->rd', hot, grad_rounded, preferred_ele...  141 us
    reduce_scatter x1, waiting for transfers between devices, per_device(): lax.psum_scatter(grad_in_weight, ('blk', 'dp'), scatter_dimension=0, tile...  139 us
    unnamed x10, waiting for transfers between devices  129 us
    reduce_scatter x1, waiting for transfers between devices, per_device(): lax.psum_scatter(grad_out_weight, ('blk', 'dp'), scatter_dimension=0, til...  71.5 us
    all_gather x1, blocking collectives, per_device(): lax.all_gather(small_params.astype(jnp.bfloat16), ('blk', 'dp'), axis=1,...  43.8 us
    all_gather x1, waiting for transfers between devices, per_device(): lax.all_gather(proj_in.astype(jnp.bfloat16), ('blk', 'dp'), axis=0, tiled...  43.8 us
    all_gather x1, blocking collectives, per_device(): lax.all_gather(proj_out.astype(jnp.bfloat16), ('blk', 'dp'), axis=0, tile...  42 us
  transfers between devices with their start and end apart: 9, of which 7 were waited for; matrix products, arithmetic and copies ran while one was open for 4% of the time, Pallas kernels for 0%

commit v1 on v0

--- a/solution.py
+++ b/solution.py
@@ -1,8 +1,11 @@
+import functools
 import math
 
 import jax
 import jax.numpy as jnp
 from jax import lax
+from jax.experimental import pallas as pl
+from jax.experimental.pallas import tpu as pltpu
 from jax.sharding import PartitionSpec as P
 
 D = 512
@@ -50,7 +53,7 @@
     return (new_moment, new_second, new_weight)
 
 
-def per_device(
+def by_events(
     item_ids,
     pos_buckets,
     time_buckets,
@@ -302,6 +305,669 @@
     )
 
 
+MESH = pl.DeviceIdType.MESH
+F32, BF16, I32 = jnp.float32, jnp.bfloat16, jnp.int32
+LANES = 128
+NN = (((1,), (0,)), ((), ()))
+NT = (((1,), (1,)), ((), ()))
+TN = (((0,), (0,)), ((), ()))
+
+
+def mm(lhs, rhs, dims=NN):
+    return lax.dot_general(lhs, rhs, dims, preferred_element_type=F32)
+
+
+def iota(shape, dim):
+    return lax.broadcasted_iota(I32, shape, dim)
+
+
+def at(index, size):
+    return pl.ds(pl.multiple_of(index * size, size), size)
+
+
+def fused_kernel(sizes, *refs):
+    nb, nz, group, items, weight_rows, tokens = sizes
+    nd = nz * 2
+    length = nb * group
+    part = D // nb
+    rows_table = items // (nb * nd)
+    (
+        ids_in, pos_in, time_in, table_in, proj_in, proj_out, small_in, out_grad_in,
+        moment_in, second_in, moment_out, second_out, moment_small, second_small,
+        layer_out, input_grad, table_grad, counts_out, logq_out,
+        new_m_in, new_s_in, new_w_in, new_m_out, new_s_out, new_w_out,
+        new_m_small, new_s_small, new_w_small,
+        send, recv, local,
+        index, column, padded, table, weight, weight_send, outw, small, small_all, cot,
+        embedded, normed, projected, gate, value, query, key, attended,
+        grad_gated, stats, fix, gated_send, gated_got, grad_att, dq, dk, dv,
+        grad_pre, part_send, part_got, stats_one, ig_send, ig_got, bias_sum, gain_sum,
+        table_sum, table_core, table_z, table_zgot, table_own, table_got,
+        gi_sum, gi_core, gi_z, gi_zgot, gi_own, gi_got,
+        go_sum, go_core, go_z, go_zgot, little, little_core, little_z, little_zgot, little_all,
+    ) = refs
+    b = lax.axis_index("blk")
+    d = lax.axis_index("dp")
+    z, core = d // 2, d % 2
+    other = 1 - core
+
+    counter = [0]
+
+    def slots(count):
+        base = counter[0]
+        counter[0] += count
+        return base
+
+    def copy(src, dst, slot, target):
+        return pltpu.make_async_remote_copy(
+            src_ref=src, dst_ref=dst, send_sem=send.at[slot], recv_sem=recv.at[slot],
+            device_id={"blk": target[0], "dp": target[1]}, device_id_type=MESH,
+        )
+
+    def blk_peer(k):
+        return (lax.rem(b + k, nb), d)
+
+    def blk_from(k):
+        return lax.rem(b + nb - k, nb)
+
+    def z_to(k):
+        return lax.rem(z + k, nz)
+
+    def z_from(k):
+        return lax.rem(z + nz - k, nz)
+
+    def z_peer(k):
+        return (b, z_to(k) * 2 + core)
+
+    core_peer = (b, z * 2 + other)
+
+    pending = []
+
+    def push(src, dst, slot, target):
+        made = copy(src, dst, slot, target)
+        made.start()
+        pending.append((src, dst, slot, target))
+
+    def arrive(dst, slot):
+        copy(dst, dst, slot, core_peer).wait_recv()
+
+    table_load = pltpu.make_async_copy(table_in, table.at[d], local.at[0])
+    table_load.start()
+    cot_load = pltpu.make_async_copy(out_grad_in, cot.at[b], local.at[1])
+    cot_load.start()
+
+    index[b] = jnp.concatenate(
+        [ids_in[...], pos_in[...], time_in[...], jnp.zeros((5, group), I32)], axis=0
+    )
+    own_rows = proj_in[...].astype(BF16)
+    for q in range(nb):
+        weight_send[q] = jnp.concatenate(
+            [own_rows[:, s * D + q * part : s * D + (q + 1) * part] for s in range(4)], axis=1
+        )
+    weight[b, d] = weight_send[b]
+    outw[b, d] = proj_out[...].astype(BF16)
+    width = small_in.shape[1]
+    spread = (iota((width, LANES), 1) == iota((width, LANES), 0) + d * width).astype(F32)
+    small_pad = jnp.concatenate([small_in[...], jnp.zeros((10, width), F32)], axis=0)
+    small[b, d] = mm(small_pad.astype(BF16), spread.astype(BF16)).astype(BF16)
+
+    barrier = pltpu.get_barrier_semaphore()
+    peers = [blk_peer(k) for k in range(1, nb)] + [z_peer(k) for k in range(1, nz)] + [core_peer]
+    for target in peers:
+        pl.semaphore_signal(
+            barrier, inc=1, device_id={"blk": target[0], "dp": target[1]}, device_id_type=MESH
+        )
+    pl.semaphore_wait(barrier, len(peers))
+
+    s_index, s_w, s_s, s_o = slots(nb), slots(nb), slots(nb), slots(nb)
+    for k in range(1, nb):
+        to = blk_peer(k)
+        push(index.at[b], index.at[b], s_index + k, to)
+        push(weight_send.at[to[0]], weight.at[b, d], s_w + k, to)
+        push(small.at[b, d], small.at[b, d], s_s + k, to)
+        push(outw.at[b, d], outw.at[b, d], s_o + k, to)
+    table_load.wait()
+    s_tz, s_tx, s_tc = slots(nz), slots(nz * nb), slots(nz * nb)
+    for k in range(1, nz):
+        push(table.at[d, b], table.at[d, b], s_tz + k, z_peer(k))
+    push(table.at[d], table.at[d], s_tc, core_peer)
+    s_wz, s_wc = slots(nz * 3), slots(nz * 3)
+    gathered = (weight, small, outw)
+    firsts = (s_w, s_s, s_o)
+    for n, (buffer, first) in enumerate(zip(gathered, firsts)):
+        for k in range(1, nb):
+            arrive(buffer.at[blk_from(k), d], first + k)
+        for k in range(1, nz):
+            push(buffer.at[:, d], buffer.at[:, d], s_wz + n * nz + k, z_peer(k))
+        push(buffer.at[:, d], buffer.at[:, d], s_wc + n * nz, core_peer)
+    for k in range(1, nz):
+        shard = z_from(k) * 2 + core
+        arrive(table.at[shard, b], s_tz + k)
+        for m in range(1, nb):
+            push(table.at[shard, b], table.at[shard, b], s_tx + k * nb + m, blk_peer(m))
+        push(table.at[shard, b], table.at[shard, b], s_tc + k * nb, core_peer)
+    for n, buffer in enumerate(gathered):
+        for k in range(1, nz):
+            shard = z_from(k) * 2 + core
+            arrive(buffer.at[:, shard], s_wz + n * nz + k)
+            push(buffer.at[:, shard], buffer.at[:, shard], s_wc + n * nz + k, core_peer)
+    for k in range(1, nz):
+        shard = z_from(k) * 2 + core
+        for m in range(1, nb):
+            arrive(table.at[shard, blk_from(m)], s_tx + k * nb + m)
+            push(table.at[shard, blk_from(m)], table.at[shard, blk_from(m)], s_tc + k * nb + m, core_peer)
+    cot_load.wait()
+    s_g = slots(nb)
+    for k in range(1, nb):
+        push(cot.at[b], cot.at[b], s_g + k, blk_peer(k))
+
+    for k in range(1, nb):
+        arrive(index.at[blk_from(k)], s_index + k)
+    padded[...] = jnp.zeros(padded.shape, F32)
+
+    def to_column(e, carry):
+        padded[0:8, :] = index[e].astype(F32)
+        column[at(e, group), :] = jnp.transpose(padded[...]).astype(I32)
+        return carry
+
+    lax.fori_loop(0, nb, to_column, 0)
+
+    for n, buffer in enumerate(gathered):
+        for k in range(0, nz):
+            arrive(buffer.at[:, z_from(k) * 2 + other], s_wc + n * nz + k)
+    arrive(table.at[z * 2 + other], s_tc)
+    for k in range(1, nz):
+        shard = z_from(k) * 2 + other
+        arrive(table.at[shard, b], s_tc + k * nb)
+        for m in range(1, nb):
+            arrive(table.at[shard, blk_from(m)], s_tc + k * nb + m)
+
+    for q in range(nb):
+        total = small[q, 0].astype(F32)
+        for r in range(1, nd):
+            total = total + small[q, r].astype(F32)
+        small_all[q] = total
+    gain_one = jnp.concatenate([small_all[q][0:1] for q in range(nb)], axis=1)
+    shift_one = jnp.concatenate([small_all[q][1:2] for q in range(nb)], axis=1)
+    mine = small_all[b]
+    gain_one_own = mine[0:1]
+    gain_two, shift_two = mine[2:3], mine[3:4]
+    pos_row, time_row = mine[4:5], mine[5:6]
+    lane = iota((1, LANES), 1)
+    low = lane < NB
+    pos_rows = (0.5 * pltpu.roll(pos_row, NB, 1), 0.5 * pos_row)
+    time_rows = (0.5 * time_row, 0.5 * pltpu.roll(time_row, NB, 1))
+    masks = (low, lane >= NB)
+
+    step = 256
+
+    def embed(t, carry):
+        rows = at(t, step)
+        picked = column[rows, 0:1]
+        hot = jnp.where(iota((step, items), 1) == picked, 1.0, 0.0).astype(BF16)
+        found = mm(hot, table[...].reshape(items, D))
+        embedded[rows, :] = found.astype(BF16)
+        mean = jnp.mean(found, axis=1, keepdims=True)
+        centered = found - mean
+        inverse = lax.rsqrt(jnp.mean(centered * centered, axis=1, keepdims=True) + norm_eps)
+        fix[rows, :] = jnp.where(lane == 0, mean, inverse)
+        ready = (centered * inverse * gain_one + shift_one).astype(BF16)
+        normed[rows, :] = ready
+        raw = mm(ready, weight[...].reshape(D, 4 * part))
+        projected[rows, :] = raw
+        act = raw * (0.5 + 0.5 * jnp.tanh(0.5 * raw))
+        gate[rows, :] = act[:, 0:part]
+        value[rows, :] = act[:, part : 2 * part].astype(BF16)
+        queries = act[:, 2 * part : 3 * part].astype(BF16).astype(F32) * (0.5 * HEAD**-0.5)
+        keys = act[:, 3 * part :].astype(BF16)
+        time_hot = jnp.where(lane == column[rows, 2:3], 1.0, 0.0)
+        pos_hot = jnp.where(lane == column[rows, 1:2] + NB, 1.0, 0.0)
+        for h in range(2):
+            query[h, rows, 0:LANES] = jnp.where(masks[h], queries, 0.0).astype(BF16)
+            query[h, rows, LANES:] = jnp.where(low, time_hot, pos_rows[h]).astype(BF16)
+            key[h, rows, 0:LANES] = keys
+            key[h, rows, LANES:] = jnp.where(low, time_rows[h], pos_hot).astype(BF16)
+        return carry
+
+    lax.fori_loop(0, length // step, embed, 0)
+    out_rows = outw[b].reshape(part, D)
+    for k in range(1, nb):
+        arrive(cot.at[blk_from(k)], s_g + k)
+
+    s_st = slots(nb * nb)
+    inv_length = 1.0 / length
+
+    def forward(r, carry):
+        i = nb - 1 - r
+        rows = at(i, group)
+        dq[...] = jnp.zeros(dq.shape, F32)
+
+        def tile(j, masked):
+            cols = at(j, group)
+            for h in range(2):
+                x = mm(query[h, rows, :], key[h, cols, :], NT)
+                w = x + x * jnp.tanh(x)
+                if masked:
+                    w = jnp.where(iota(w.shape, 0) >= iota(w.shape, 1), w, 0.0)
+                dq[h, :, 0:LANES] += mm(w.astype(BF16), value[cols, :])
+
+        def full(j, inner):
+            tile(j, False)
+            return inner
+
+        lax.fori_loop(0, i, full, 0)
+        tile(i, True)
+        att = jnp.where(low, dq[0, :, 0:LANES], dq[1, :, 0:LANES]) * inv_length
+        attended[rows, :] = att
+        gg = mm(cot[i], out_rows, NT)
+        grad_gated[rows, :] = gg
+        g = gg * gate[rows, :] * gain_two
+        mean = jnp.mean(att, axis=1, keepdims=True)
+        centered = att - mean
+        square = jnp.sum(centered * centered, axis=1, keepdims=True)
+        sum_g = jnp.sum(g, axis=1, keepdims=True)
+        sum_ga = jnp.sum(g * centered, axis=1, keepdims=True)
+        packed = jnp.where(
+            lane == 0, mean, jnp.where(lane == 1, square, jnp.where(lane == 2, sum_g, sum_ga))
+        )
+        stats[b, i] = jnp.transpose(packed)[0:8]
+        for k in range(1, nb):
+            copy(stats.at[b, i], stats.at[b, i], s_st + i * nb + k, blk_peer(k)).start()
+        return carry
+
+    lax.fori_loop(0, nb, forward, 0)
+
+    s_ps, s_s1 = slots(nb * nb), slots(nb * nb)
+    dk[...] = jnp.zeros(dk.shape, F32)
+    dv[...] = jnp.zeros(dv.shape, F32)
+    bias_sum[...] = jnp.zeros(bias_sum.shape, F32)
+    gain_sum[...] = jnp.zeros(gain_sum.shape, F32)
+
+    def backward(r, carry):
+        i = nb - 1 - r
+        rows = at(i, group)
+        for k in range(1, nb):
+            arrive(stats.at[blk_from(k), i], s_st + i * nb + k)
+        every = [stats[q, i] for q in range(nb)]
+        mean = sum(s[0:1] for s in every) * (1.0 / nb)
+        square = sum(s[1:2] + part * (s[0:1] - mean) * (s[0:1] - mean) for s in every)
+        inverse = lax.rsqrt(square * (1.0 / D) + norm_eps)
+        mean_g = sum(s[2:3] for s in every) * (1.0 / D)
+        cross = inverse * sum(s[3:4] + (s[0:1] - mean) * s[2:3] for s in every) * (1.0 / D)
+        padded[0:1, :] = mean
+        padded[1:2, :] = inverse
+        padded[2:3, :] = mean_g
+        padded[3:4, :] = cross
+        turned = jnp.transpose(padded[...])
+        inverse = turned[:, 1:2]
+        hat = (attended[rows, :] - turned[:, 0:1]) * inverse
+        normal = hat * gain_two + shift_two
+        gated_send[i] = (normal * gate[rows, :]).astype(BF16)
+        gg = grad_gated[rows, :]
+        grad_u = gg * normal
+        grad_norm = gg * gate[rows, :]
+        gain_sum[2:3, :] += jnp.sum(grad_norm * hat, axis=0, keepdims=True)
+        gain_sum[3:4, :] += jnp.sum(grad_norm, axis=0, keepdims=True)
+        ga = (grad_norm * gain_two - turned[:, 2:3] - hat * turned[:, 3:4]) * inverse
+        for h in range(2):
+            grad_att[h] = jnp.where(masks[h], ga, 0.0).astype(BF16)
+        dq[...] = jnp.zeros(dq.shape, F32)
+
+        def tile(j, masked):
+            cols = at(j, group)
+            for h in range(2):
+                x = mm(key[h, cols, :], query[h, rows, :], NT)
+                t = jnp.tanh(x)
+                u = 1.0 + t
+                w = x * u
+                slope = u * (1.0 + x * (1.0 - t))
+                if masked:
+                    allowed = iota(w.shape, 0) <= iota(w.shape, 1)
+                    w = jnp.where(allowed, w, 0.0)
+                    slope = jnp.where(allowed, slope, 0.0)
+                dw = mm(value[cols, :], grad_att[h], NT)
+                graw = (dw * slope).astype(BF16)
+                dv[j] += mm(w.astype(BF16), grad_att[h])
+                back = mm(graw, query[h, rows, :])
+                dk[j] += back[:, 0:LANES]
+                bias_sum[h : h + 1, :] += jnp.sum(back[:, LANES:], axis=0, keepdims=True)
+                dq[h] += mm(graw, key[h, cols, :], TN)
+
+        def full(j, inner):
+            tile(j, False)
+            return inner
+
+        lax.fori_loop(0, i, full, 0)
+        tile(i, True)
+        for h in range(2):
+            bias_sum[2 + h : 3 + h, :] += jnp.sum(dq[h, :, LANES:], axis=0, keepdims=True)
+        grad_q = jnp.where(low, dq[0, :, 0:LANES], dq[1, :, 0:LANES]) * (
+            0.5 * inv_length * HEAD**-0.5
+        )
+        raw = projected[rows, :]
+        logistic = 0.5 + 0.5 * jnp.tanh(0.5 * raw)
+        slope = logistic * (1.0 + raw * (1.0 - logistic))
+        acts = jnp.concatenate([grad_u, dv[i] * inv_length, grad_q, dk[i] * inv_length], axis=1)
+        pre = (acts * slope).astype(BF16)
+        grad_pre[rows, :] = pre
+        partial = mm(pre, weight[...].reshape(D, 4 * part), NT)
+        scaled = partial * gain_one
+        first = jnp.sum(scaled, axis=1, keepdims=True)
+        mean_one, inverse_one = fix[rows, 0:1], fix[rows, 1:2]
+        hat_one = (embedded[rows, :].astype(F32) - mean_one) * inverse_one
+        second = jnp.sum(scaled * hat_one, axis=1, keepdims=True)
+        stats_one[b, i] = jnp.transpose(jnp.where(lane == 0, first, second))[0:8]
+        for q in range(nb):
+            part_send[q, i] = partial[:, q * part : (q + 1) * part].astype(BF16)
+        for k in range(1, nb):
+            to = blk_peer(k)
+            copy(part_send.at[to[0], i], part_got.at[b, i], s_ps + i * nb + k, to).start()
+            copy(stats_one.at[b, i], stats_one.at[b, i], s_s1 + i * nb + k, to).start()
+        part_got[b, i] = part_send[b, i]
+        return carry
+
+    lax.fori_loop(0, nb, backward, 0)
+
+    s_gt = slots(nb)
+    for k in range(1, nb):
+        to = blk_peer(k)
+        push(gated_send.at[to[0]], gated_got.at[b], s_gt + k, to)
+    gated_got[b] = gated_send[b]
+
+    def core_stage(total, landing, base):
+        for k in range(nz):
+            push(total.at[:, k * 2 + other], landing.at[k], base + k, core_peer)
+
+    def core_sum(total, landing, outgoing, base):
+        for k in range(nz):
+            arrive(landing.at[k], base + k)
+            outgoing[k] = (total[:, k * 2 + core].astype(F32) + landing[k].astype(F32)).astype(BF16)
+
+    def z_stage(outgoing, landing, base):
+        for k in range(1, nz):
+            push(outgoing.at[z_to(k)], landing.at[k], base + k, z_peer(k))
+
+    def z_sum(outgoing, landing, base):
+        total = outgoing[z].astype(F32)
+        for k in range(1, nz):
+            arrive(landing.at[k], base + k)
+            total = total + landing[k].astype(F32)
+        return total
+
+    s_gic, s_giz, s_gix = slots(nz), slots(nz), slots(nb)
+    s_goc, s_goz = slots(nz), slots(nz)
+
+    gated_all = gated_send[...].reshape(length, part)
+    go_sum[...] = mm(gated_all, cot[...].reshape(length, D), TN).astype(BF16).reshape(go_sum.shape)
+    core_stage(go_sum, go_core, s_goc)
+
+    def weight_grad(t, carry):
+        cols = at(t, LANES)
+        got = mm(normed[:, cols], grad_pre[...], TN).astype(BF16)
+        gi_sum[t] = got.reshape(gi_sum.shape[1:])
+        return carry
+
+    lax.fori_loop(0, nb, weight_grad, 0)
+    core_stage(gi_sum, gi_core, s_gic)
+
+    s_ig = slots(nb)
+
+    def input_part(r, carry):
+        i = nb - 1 - r
+        rows = at(i, group)
+        for k in range(1, nb):
+            arrive(part_got.at[blk_from(k), i], s_ps + i * nb + k)
+            arrive(stats_one.at[blk_from(k), i], s_s1 + i * nb + k)
+        total = sum(part_got[q, i].astype(F32) for q in range(nb))
+        row = sum(stats_one[q, i] for q in range(nb)) * (1.0 / D)
+        padded[0:8, :] = row
+        turned = jnp.transpose(padded[...])
+        mean_one, inverse_one = fix[rows, 0:1], fix[rows, 1:2]
+        mycols = at(b, part)
+        hat_one = (embedded[rows, mycols].astype(F32) - mean_one) * inverse_one
+        gain_sum[0:1, :] += jnp.sum(total * hat_one, axis=0, keepdims=True)
+        gain_sum[1:2, :] += jnp.sum(total, axis=0, keepdims=True)
+        back = (total * gain_one_own - turned[:, 0:1] - hat_one * turned[:, 1:2]) * inverse_one
+        ig_send[i] = (cot[i, :, mycols].astype(F32) + back).astype(BF16)
+        return carry
+
+    lax.fori_loop(0, nb, input_part, 0)
+    for k in range(1, nb):
+        to = blk_peer(k)
+        push(ig_send.at[to[0]], ig_got.at[b], s_ig + k, to)
+    ig_got[b] = ig_send[b]
+
+    s_tgc, s_tgz, s_tgx = slots(nz), slots(nz), slots(nb)
+
+    def table_part(t, carry):
+        picked = jnp.concatenate([index[e][0:1] for e in range(nb)], axis=1)
+        hot = jnp.where(iota((step, length), 0) + t * step == picked, 1.0, 0.0).astype(BF16)
+        got = mm(hot, ig_send[...].reshape(length, part)).astype(BF16)
+        table_sum[t // (items // nb // step), at(t % (items // nb // step), step // rows_table)] = (
+            got.reshape(step // rows_table, rows_table, part)
+        )
+        return carry
+
+    lax.fori_loop(0, items // step, table_part, 0)
+    core_stage(table_sum, table_core, s_tgc)
+
+    s_lc, s_lz = slots(1), slots(nz)
+    own_items = items // nb
+
+    def count(t, carry):
+        picked = column[at(t, step), 0:1]
+        hit = jnp.where(iota((step, own_items), 1) + b * own_items == picked, 1.0, 0.0)
+        return carry + jnp.sum(hit, axis=0, keepdims=True)
+
+    counted = lax.fori_loop(0, length // step, count, jnp.zeros((1, own_items), F32))
+    time_grad = jnp.where(low, bias_sum[0:1, :], pltpu.roll(bias_sum[1:2, :], NB, 1))
+    pos_grad = jnp.where(low, pltpu.roll(bias_sum[2:3, :], NB, 1), bias_sum[3:4, :])
+    halved = 0.5 * inv_length
+    little[...] = jnp.zeros(little.shape, F32)
+    little[0:4, :] = gain_sum[0:4, :]
+    little[4:5, :] = pos_grad * halved
+    little[5:6, :] = time_grad * halved
+    for q in range(own_items // LANES):
+        little[8 + q : 9 + q, :] = counted[:, q * LANES : (q + 1) * LANES]
+    push(little, little_core, s_lc, core_peer)
+
+    core_sum(go_sum, go_core, go_z, s_goc)
+    z_stage(go_z, go_zgot, s_goz)
+    core_sum(gi_sum, gi_core, gi_z, s_gic)
+    z_stage(gi_z, gi_zgot, s_giz)
+    arrive(little_core, s_lc)
+    little_z[...] = little[...] + little_core[...]
+    for k in range(1, nz):
+        push(little_z, little_zgot.at[k], s_lz + k, z_peer(k))
+    core_sum(table_sum, table_core, table_z, s_tgc)
+    z_stage(table_z, table_zgot, s_tgz)
+
+    for k in range(1, nb):
+        arrive(gated_got.at[blk_from(k)], s_gt + k)
+    result = embedded[at(b, group), :].astype(F32)
+    for q in range(nb):
+        result = result + mm(gated_got[q], outw[q].reshape(part, D))
+    layer_out[...] = result.astype(BF16)
+
+    gi_own[...] = z_sum(gi_z, gi_zgot, s_giz)
+    for k in range(1, nb):
+        to = blk_peer(k)
+        push(gi_own.at[to[0]], gi_got.at[b], s_gix + k, to)
+    gi_got[b] = gi_own[b]
+    table_own[...] = z_sum(table_z, table_zgot, s_tgz)
+    for k in range(1, nb):
+        to = blk_peer(k)
+        push(table_own.at[to[0]], table_got.at[b], s_tgx + k, to)
+    table_got[b] = table_own[b]
+
+    grad_out = z_sum(go_z, go_zgot, s_goz)[0]
+    new_m_out[...], new_s_out[...], new_w_out[...] = adam_update(
+        proj_out[...], grad_out, moment_out[...], second_out[...], rate_out
+    )
+    totals = little_z[...]
+    for k in range(1, nz):
+        arrive(little_zgot.at[k], s_lz + k)
+        totals = totals + little_zgot[k]
+    little_all[...] = totals
+    shifted = pltpu.roll(little_all[0:8, :], lax.rem(LANES - d * width, LANES), 1)[0:6, 0:width]
+    new_m_small[...], new_s_small[...], new_w_small[...] = adam_update(
+        small_in[...], shifted, moment_small[...], second_small[...], rate_small
+    )
+    per_row = LANES // rows_table
+    count_row = little_all[pl.ds(8 + d // per_row, 1), :]
+    count_row = pltpu.roll(
+        jnp.broadcast_to(count_row, (8, LANES)),
+        lax.rem(LANES - lax.rem(d, per_row) * rows_table, LANES), 1,
+    )[0:1, 0:rows_table]
+    counts_out[...] = count_row
+    logq_out[...] = jnp.log(jnp.maximum(count_row, 1.0) * (1.0 / tokens))
+
+    for k in range(1, nb):
+        arrive(gi_got.at[blk_from(k)], s_gix + k)
+    grad_in = jnp.concatenate(
+        [gi_got[q][:, s * part : (s + 1) * part] for s in range(4) for q in range(nb)], axis=1
+    )
+    new_m_in[...], new_s_in[...], new_w_in[...] = adam_update(
+        proj_in[...], grad_in, moment_in[...], second_in[...], rate_in
+    )
+    for k in range(1, nb):
+        arrive(ig_got.at[blk_from(k)], s_ig + k)
+    for q in range(nb):
+        input_grad[:, q * part : (q + 1) * part] = ig_got[q].astype(F32)
+    for k in range(1, nb):
+        arrive(table_got.at[blk_from(k)], s_tgx + k)
+    for q in range(nb):
+        table_grad[:, q * part : (q + 1) * part] = table_got[q]
+
+    for args in pending:
+        copy(*args).wait_send()
+
+    def drain(i, carry):
+        for k in range(1, nb):
+            to = blk_peer(k)
+            copy(stats.at[b, i], stats.at[b, i], s_st + i * nb + k, to).wait_send()
+            copy(part_send.at[to[0], i], part_got.at[b, i], s_ps + i * nb + k, to).wait_send()
+            copy(stats_one.at[b, i], stats_one.at[b, i], s_s1 + i * nb + k, to).wait_send()
+        return carry
+
+    lax.fori_loop(0, nb, drain, 0)
+    assert counter[0] <= send.shape[0], counter[0]
+
+
+def fused(sizes, args):
+    nb, nz, group, items, weight_rows, tokens = sizes
+    nd = nz * 2
+    length = nb * group
+    part = D // nb
+    rows_table = items // (nb * nd)
+    (
+        item_ids, pos_buckets, time_buckets, item_table, proj_in, proj_out, small_params, out_grad,
+        moment_in, second_in, moment_out, second_out, moment_small, second_small,
+    ) = args
+    width = small_params.shape[1]
+    shape = jax.ShapeDtypeStruct
+    outs = [
+        shape((group, D), BF16), shape((group, D), F32), shape((rows_table, D), F32),
+        shape((1, rows_table), F32), shape((1, rows_table), F32),
+        *[shape(proj_in.shape, F32)] * 3, *[shape(proj_out.shape, F32)] * 3,
+        *[shape(small_params.shape, F32)] * 3,
+    ]
+    vm = pltpu.VMEM
+    scratch = [
+        pltpu.SemaphoreType.DMA((192,)), pltpu.SemaphoreType.DMA((192,)), pltpu.SemaphoreType.DMA((2,)),
+        vm((nb, 8, group), I32),
+        vm((length, LANES), I32),
+        vm((LANES, group), F32),
+        vm((nd, nb, rows_table, D), BF16),
+        vm((nb, nd, weight_rows, 4 * part), BF16),
+        vm((nb, weight_rows, 4 * part), BF16),
+        vm((nb, nd, weight_rows, D), BF16),
+        vm((nb, nd, 16, LANES), BF16),
+        vm((nb, 16, LANES), F32),
+        vm((nb, group, D), BF16),
+        vm((length, D), BF16),
+        vm((length, D), BF16),
+        vm((length, 4 * part), F32),
+        vm((length, part), F32),
+        vm((length, part), BF16),
+        vm((2, length, 2 * LANES), BF16),
+        vm((2, length, 2 * LANES), BF16),
+        vm((length, part), F32),
+        vm((length, part), F32),
+        vm((nb, nb, 8, group), F32),
+        vm((length, LANES), F32),
+        vm((nb, group, part), BF16),
+        vm((nb, group, part), BF16),
+        vm((2, group, part), BF16),
+        vm((2, group, 2 * LANES), F32),
+        vm((nb, group, part), F32),
+        vm((nb, group, part), F32),
+        vm((length, 4 * part), BF16),
+        vm((nb, nb, group, part), BF16),
+        vm((nb, nb, group, part), BF16),
+        vm((nb, nb, 8, group), F32),
+        vm((nb, group, part), BF16),
+        vm((nb, group, part), BF16),
+        vm((8, LANES), F32),
+        vm((8, LANES), F32),
+        vm((nb, nd, rows_table, part), BF16),
+        vm((nz, nb, rows_table, part), BF16),
+        vm((nz, nb, rows_table, part), BF16),
+        vm((nz, nb, rows_table, part), BF16),
+        vm((nb, rows_table, part), F32),
+        vm((nb, rows_table, part), F32),
+        vm((nb, nd, weight_rows, 4 * part), BF16),
+        vm((nz, nb, weight_rows, 4 * part), BF16),
+        vm((nz, nb, weight_rows, 4 * part), BF16),
+        vm((nz, nb, weight_rows, 4 * part), BF16),
+        vm((nb, weight_rows, 4 * part), F32),
+        vm((nb, weight_rows, 4 * part), F32),
+        vm((1, nd, weight_rows, D), BF16),
+        vm((nz, 1, weight_rows, D), BF16),
+        vm((nz, 1, weight_rows, D), BF16),
+        vm((nz, 1, weight_rows, D), BF16),
+        vm((16, LANES), F32), vm((16, LANES), F32), vm((16, LANES), F32), vm((nz, 16, LANES), F32),
+        vm((16, LANES), F32),
+    ]
+    whole, far = pl.BlockSpec(memory_space=pltpu.VMEM), pl.BlockSpec(memory_space=pl.ANY)
+    got = pl.pallas_call(
+        functools.partial(fused_kernel, sizes),
+        out_shape=outs,
+        in_specs=[whole] * 3 + [far] + [whole] * 3 + [far] + [whole] * 6,
+        out_specs=[whole] * len(outs),
+        scratch_shapes=scratch,
+        compiler_params=pltpu.CompilerParams(
+            collective_id=0, has_side_effects=True, vmem_limit_bytes=60 * 2**20
+        ),
+        name="hstu_step",
+    )(
+        item_ids, pos_buckets, time_buckets,
+        item_table.reshape(nb, item_table.shape[0] // nb, D),
+        proj_in, proj_out, small_params, out_grad.reshape(group, D),
+        moment_in, second_in, moment_out, second_out, moment_small, second_small,
+    )
+    return (
+        got[0].reshape(out_grad.shape), got[1].reshape(out_grad.shape), got[2],
+        got[3].reshape(rows_table), got[4].reshape(rows_table), *got[5:],
+    )
+
+
+def per_device(*args):
+    item_ids, item_table, proj_in, small_params = args[0], args[3], args[4], args[6]
+    seq_count, group = item_ids.shape
+    nb, nd = lax.axis_size("blk"), lax.axis_size("dp")
+    items = item_table.shape[0] * nd
+    by_heads = (
+        seq_count == 1 and nd % 2 == 0 and D // nb == LANES and group % 256 == 0
+        and items <= 2048 and items // (nb * nd) % 16 == 0 and proj_in.shape[0] % 16 == 0
+        and small_params.shape[1] * nd == LANES
+    )
+    if by_heads:
+        sizes = (nb, nd // 2, group, items, proj_in.shape[0], nd * nb * group)
+        return fused(sizes, args)
+    return by_events(*args)
+
+
 def solution(mesh):
     placed = (
         P("dp", "blk"),

time: 971 us -> 135 us (0.14)
  waiting for transfers between devices: 699 us -> 0 us
  blocking collectives: 133 us -> 0 us
  Pallas kernels: 0 us -> 122 us
  matrix products: 51.7 us -> 0 us
  local copies, waits for them, and re-layouts: 42.9 us -> 11.6 us
  other arithmetic: 22.7 us -> 0 us
  between operations: 14.3 us -> 0.69 us
    reduce_scatter x4 -> x0, waiting for transfers between devices: 505 us -> none  [the longest x1 154 us: per_device(): kv_own = lax.psum_scatter(kv_terms, 'blk', scatter_dimension=1, tiled=True)]
    unnamed x10 -> x0, waiting for transfers between devices: 129 us -> none
    pallas_call x0 -> x1, Pallas kernels: none -> 122 us  [fused(): pl.pallas_call(functools.partial(fused_kernel, sizes), out_shape=outs, in...]
    all_gather x3 -> x0, blocking collectives: 93.8 us -> none  [the longest x1 43.8 us: per_device(): lax.all_gather(small_params.astype(jnp.bfloat16), ('blk', 'dp'), axis=1,...]
    all_gather x4 -> x0, waiting for transfers between devices: 64.9 us -> none  [the longest x1 43.8 us: per_device(): lax.all_gather(proj_in.astype(jnp.bfloat16), ('blk', 'dp'), axis=0, tiled...]
    dot_general x19 -> x0, matrix products: 51.7 us -> none  [the longest x1 6.78 us: per_device(): projected = jnp.dot(normed, copy_in, preferred_element_type=jnp.float32)]
    unnamed x1 -> x0, blocking collectives: 39.4 us -> none
    dynamic_update_slice x8 -> x0, local copies, waits for them, and re-layouts: 20.2 us -> none  [per_device(): lax.scan(back_step, back_init, jnp.arange(length // rows_back, dtype=jnp....]
  transfers between devices with their start and end apart: 9 -> 0, of which waited for: 7 -> 0; matrix products, arithmetic and copies ran while one was open for 4% -> 0% of each run, Pallas kernels for 0% -> 0%
where the time goes in v1:
time: 135 us
  Pallas kernels  122 us (90%)
  local copies, waits for them, and re-layouts  11.6 us (9%)
    pallas_call x1, Pallas kernels, fused(): pl.pallas_call(functools.partial(fused_kernel, sizes), out_shape=outs, in...  122 us
    unnamed x40, local copies, waits for them, and re-layouts  11.6 us

profile of v1, /device:TPU:0, one launch (start us, length us, event | category | flops | bytes accessed | tf_op | source)
XLA Modules:
  0.0 134.8 jit_solution(9484937207526325168)
XLA Ops:
  0.7 122.5 %hstu_step.1 = (bf16[512,512]{1,0:T(8,128)(2,1)}, f32[512,512]{1,0:T(8,128)}, f32[64,512]{1,0:T(8,128)}, f32[1,64]{1,0:T(1,128)}, f32[1,64]{1,0:T(1,128)}, /*ind...) custom-call(s32[1,512]{1,0:T(1,128)} %refs_0_.1, ...), custom_call_target="tpu_custom_call" | custom-call | tf_op jit(solution)/shard_map/hstu_step/pallas_call | solution.py:933
  123.1 0.0 copy-start
  123.1 2.0 %copy.42 = bf16[1,512,512]{2,1,0:T(8,128)(2,1)} copy(bf16[1,512,512]{2,1,0:T(8,128)(2,1)} %bitcast.8) | data formatting | bytes 1048576
  125.1 0.0 copy-done
  125.1 0.0 copy-start.4
  125.1 1.0 copy.43
  126.1 0.1 copy-done.4
  126.1 0.0 copy-start.12
  126.1 0.0 copy-start.3
  126.1 0.7 copy.44
  126.8 0.0 copy-done.12
  126.8 0.0 copy-start.11
  126.8 0.5 copy.45
  127.3 0.1 copy-done.11
  127.4 0.5 copy.46
  127.9 0.0 copy-done.3
  127.9 0.0 copy-start.2
  127.9 0.7 copy.47
  128.6 0.3 copy-done.2
  128.9 0.0 copy-start.1
  128.9 0.7 copy.48
  129.6 0.3 copy-done.1
  129.8 0.0 copy-start.7
  129.8 0.7 copy.49
  130.5 0.1 copy-done.7
  130.6 0.0 copy-start.6
  130.6 0.6 copy.50
  131.2 0.2 copy-done.6
  131.4 0.0 copy-start.5
  131.4 0.6 copy.51
  132.0 0.2 copy-done.5
  132.1 0.0 copy-start.10
  132.1 0.6 copy.52
  132.8 0.1 copy-done.10
  132.8 0.0 copy-start.9
  132.8 0.6 copy.53
  133.4 0.1 copy-done.9
  133.5 0.0 copy-start.8
  133.5 0.6 copy.54
  134.1 0.1 copy-done.8
  134.2 0.6 copy.55
Async XLA Ops:
  123.1 2.0 %copy-start = (f32[512,512]{1,0:T(8,128)S(1)}, f32[512,512]{1,0:T(8,128)}, u32[]{:S(2)}) copy-start(f32[512,512]{1,0:T(8,128)} %get-tuple-element.29) | copy-start | bytes 3145732
  125.1 1.0 copy-start.4
  126.1 0.7 copy-start.12
  126.1 1.8 %copy-start.3 = (f32[16,2048]{1,0:T(8,128)S(1)}, f32[16,2048]{1,0:T(8,128)}, u32[]{:S(2)}) copy-start(f32[16,2048]{1,0:T(8,128)} %get-tuple-element.61) | copy-start | bytes 393220
  126.8 0.7 copy-start.11
  127.9 1.0 copy-start.2
  128.9 1.0 copy-start.1
  129.8 0.8 copy-start.7
  130.6 0.8 copy-start.6
  131.4 0.8 copy-start.5
  132.1 0.7 copy-start.10
  132.8 0.7 copy-start.9
  133.5 0.7 copy-start.8

commit v2 on v1

--- a/solution.py
+++ b/solution.py
@@ -333,18 +333,15 @@
     rows_table = items // (nb * nd)
     (
         ids_in, pos_in, time_in, table_in, proj_in, proj_out, small_in, out_grad_in,
-        moment_in, second_in, moment_out, second_out, moment_small, second_small,
-        layer_out, input_grad, table_grad, counts_out, logq_out,
-        new_m_in, new_s_in, new_w_in, new_m_out, new_s_out, new_w_out,
-        new_m_small, new_s_small, new_w_small,
+        layer_out, input_out, table_out, grad_in_out, grad_out_out, little_out,
         send, recv, local,
-        index, column, padded, table, weight, weight_send, outw, small, small_all, cot,
+        index, column, padded, table, weight, weight_send, outw, small_send, small, small_all, cot,
         embedded, normed, projected, gate, value, query, key, attended,
         grad_gated, stats, fix, gated_send, gated_got, grad_att, dq, dk, dv,
         grad_pre, part_send, part_got, stats_one, ig_send, ig_got, bias_sum, gain_sum,
         table_sum, table_core, table_z, table_zgot, table_own, table_got,
         gi_sum, gi_core, gi_z, gi_zgot, gi_own, gi_got,
-        go_sum, go_core, go_z, go_zgot, little, little_core, little_z, little_zgot, little_all,
+        go_sum, go_core, go_z, go_zgot, little, little_core, little_z, little_zgot,
     ) = refs
     b = lax.axis_index("blk")
     d = lax.axis_index("dp")
@@ -358,9 +355,10 @@
         counter[0] += count
         return base
 
-    def copy(src, dst, slot, target):
+    def copy(src, dst, slot, target, landing=None):
         return pltpu.make_async_remote_copy(
-            src_ref=src, dst_ref=dst, send_sem=send.at[slot], recv_sem=recv.at[slot],
+            src_ref=src, dst_ref=dst, send_sem=send.at[slot],
+            recv_sem=recv.at[slot if landing is None else landing],
             device_id={"blk": target[0], "dp": target[1]}, device_id_type=MESH,
         )
 
@@ -383,10 +381,29 @@
 
     pending = []
 
-    def push(src, dst, slot, target):
-        made = copy(src, dst, slot, target)
-        made.start()
-        pending.append((src, dst, slot, target))
+    def push(src, dst, slot, target, landing=None, where=None):
+        def start():
+            copy(src, dst, slot, target, landing).start()
+
+        if where is None:
+            start()
+        else:
+            pl.when(where)(start)
+        pending.append((where, src, dst, slot, target))
+
+    near = (z + 1 - 2 * (z % 2), 2 - z // 2, 3 * (1 - z // 2))
+
+    def chain_start(ref, base):
+        for n, (beside, there) in enumerate(((z - 1, z > 0), (z + 1, z < nz - 1))):
+            to = jnp.clip(beside, 0, nz - 1)
+            push(ref, ref, base + n, (b, to * 2 + core), base + z, there)
+
+    def chain_next(ref, base, n):
+        arrive(ref, base + near[n])
+        beyond = jnp.where(near[n] < z, z + 1, z - 1)
+        there = jnp.logical_and(beyond >= 0, beyond < nz)
+        to = jnp.clip(beyond, 0, nz - 1)
+        push(ref, ref, base + 2 + n, (b, to * 2 + core), base + near[n], there)
 
     def arrive(dst, slot):
         copy(dst, dst, slot, core_peer).wait_recv()
@@ -407,9 +424,9 @@
     weight[b, d] = weight_send[b]
     outw[b, d] = proj_out[...].astype(BF16)
     width = small_in.shape[1]
-    spread = (iota((width, LANES), 1) == iota((width, LANES), 0) + d * width).astype(F32)
+    spread = (iota((width, LANES), 1) == iota((width, LANES), 0) + b * width).astype(F32)
     small_pad = jnp.concatenate([small_in[...], jnp.zeros((10, width), F32)], axis=0)
-    small[b, d] = mm(small_pad.astype(BF16), spread.astype(BF16)).astype(BF16)
+    small_send[b] = mm(small_pad.astype(BF16), spread.astype(BF16)).astype(BF16)
 
     barrier = pltpu.get_barrier_semaphore()
     peers = [blk_peer(k) for k in range(1, nb)] + [z_peer(k) for k in range(1, nz)] + [core_peer]
@@ -419,47 +436,51 @@
         )
     pl.semaphore_wait(barrier, len(peers))
 
-    s_index, s_w, s_s, s_o = slots(nb), slots(nb), slots(nb), slots(nb)
+    s_index, s_w, s_s = slots(nb), slots(nb), slots(nb)
     for k in range(1, nb):
         to = blk_peer(k)
         push(index.at[b], index.at[b], s_index + k, to)
         push(weight_send.at[to[0]], weight.at[b, d], s_w + k, to)
-        push(small.at[b, d], small.at[b, d], s_s + k, to)
-        push(outw.at[b, d], outw.at[b, d], s_o + k, to)
+        push(small_send.at[b], small_send.at[b], s_s + k, to)
     table_load.wait()
-    s_tz, s_tx, s_tc = slots(nz), slots(nz * nb), slots(nz * nb)
-    for k in range(1, nz):
-        push(table.at[d, b], table.at[d, b], s_tz + k, z_peer(k))
-    push(table.at[d], table.at[d], s_tc, core_peer)
-    s_wz, s_wc = slots(nz * 3), slots(nz * 3)
-    gathered = (weight, small, outw)
-    firsts = (s_w, s_s, s_o)
-    for n, (buffer, first) in enumerate(zip(gathered, firsts)):
-        for k in range(1, nb):
-            arrive(buffer.at[blk_from(k), d], first + k)
+    s_tz, s_tx, s_tc = slots(nz + 2), slots(nz * nb), slots(nz * nb)
+    chain_start(table.at[d, b], s_tz)
+    push(table.at[d], table.at[d], s_tc, core_peer, s_tc + z * nb)
+    cot_load.wait()
+    s_g = slots(6)
+    x_peer, y_peer = (b // 2 * 2 + 1 - b % 2, d), (lax.rem(b + 2, nb), d)
+    halves = (slice(0, group // 2), slice(group // 2, group))
+    sides = (x_peer, y_peer)
+
+    def cot_half(owner, n):
+        return cot.at[owner, halves[n]]
+
+    def own_half(n):
+        for m in range(2):
+            push(cot_half(b, n), cot_half(b, n), s_g + 2 * n + m, sides[m])
+
+    s_wz, s_wc = slots(3 * (nz + 2)), slots(3 * nz)
+
+    def shard_of(n, slot):
+        return (weight.at[:, slot], small.at[slot], outw.at[b, slot])[n]
+
+    def shard_start(n):
         for k in range(1, nz):
-            push(buffer.at[:, d], buffer.at[:, d], s_wz + n * nz + k, z_peer(k))
-        push(buffer.at[:, d], buffer.at[:, d], s_wc + n * nz, core_peer)
-    for k in range(1, nz):
-        shard = z_from(k) * 2 + core
-        arrive(table.at[shard, b], s_tz + k)
-        for m in range(1, nb):
-            push(table.at[shard, b], table.at[shard, b], s_tx + k * nb + m, blk_peer(m))
-        push(table.at[shard, b], table.at[shard, b], s_tc + k * nb, core_peer)
-    for n, buffer in enumerate(gathered):
-        for k in range(1, nz):
-            shard = z_from(k) * 2 + core
-            arrive(buffer.at[:, shard], s_wz + n * nz + k)
-            push(buffer.at[:, shard], buffer.at[:, shard], s_wc + n * nz + k, core_peer)
-    for k in range(1, nz):
-        shard = z_from(k) * 2 + core
-        for m in range(1, nb):
-            arrive(table.at[shard, blk_from(m)], s_tx + k * nb + m)
-            push(table.at[shard, blk_from(m)], table.at[shard, blk_from(m)], s_tc + k * nb + m, core_peer)
-    cot_load.wait()
-    s_g = slots(nb)
-    for k in range(1, nb):
-        push(cot.at[b], cot.at[b], s_g + k, blk_peer(k))
+            push(shard_of(n, d), shard_of(n, d), s_wz + n * (nz + 2) + k, z_peer(k), s_wz + n * (nz + 2) + z)
+        push(shard_of(n, d), shard_of(n, d), s_wc + n * nz, core_peer, s_wc + n * nz + z)
+
+    def shard_next(n, m):
+        ref = shard_of(n, near[m] * 2 + core)
+        arrive(ref, s_wz + n * (nz + 2) + near[m])
+        push(ref, ref, s_wc + n * nz + 1 + m, core_peer, s_wc + n * nz + near[m])
+
+    for k in range(1, nb):
+        arrive(weight.at[blk_from(k), d], s_w + k)
+    shard_start(0)
+    for k in range(1, nb):
+        arrive(small_send.at[blk_from(k)], s_s + k)
+    small[d] = sum(small_send[q].astype(F32) for q in range(nb)).astype(BF16)
+    shard_start(1)
 
     for k in range(1, nb):
         arrive(index.at[blk_from(k)], s_index + k)
@@ -472,20 +493,86 @@
 
     lax.fori_loop(0, nb, to_column, 0)
 
-    for n, buffer in enumerate(gathered):
-        for k in range(0, nz):
-            arrive(buffer.at[:, z_from(k) * 2 + other], s_wc + n * nz + k)
-    arrive(table.at[z * 2 + other], s_tc)
-    for k in range(1, nz):
-        shard = z_from(k) * 2 + other
-        arrive(table.at[shard, b], s_tc + k * nb)
+    step = 256
+
+    def table_over_z(n):
+        shard = near[n] * 2 + core
+        chain_next(table.at[shard, b], s_tz, n)
         for m in range(1, nb):
-            arrive(table.at[shard, blk_from(m)], s_tc + k * nb + m)
-
+            push(
+                table.at[shard, b], table.at[shard, b], s_tx + n * nb + m, blk_peer(m),
+                s_tx + near[n] * nb + m,
+            )
+        push(
+            table.at[shard, b], table.at[shard, b], s_tc + (n + 1) * nb, core_peer,
+            s_tc + near[n] * nb,
+        )
+
+    def table_over_blk(n):
+        shard = near[n] * 2 + core
+        for m in range(1, nb):
+            quarter = table.at[shard, blk_from(m)]
+            arrive(quarter, s_tx + near[n] * nb + m)
+            push(quarter, quarter, s_tc + (n + 1) * nb + m, core_peer, s_tc + near[n] * nb + m)
+
+    def table_over_core(n):
+        shard = near[n] * 2 + other
+        arrive(table.at[shard, b], s_tc + near[n] * nb)
+        for m in range(1, nb):
+            arrive(table.at[shard, blk_from(m)], s_tc + near[n] * nb + m)
+
+    def picked_rows(rows, at_z):
+        picked = column[rows, 0:1] - at_z * (items // nz)
+        hot = jnp.where(iota((step, items // nz), 1) == picked, 1.0, 0.0).astype(BF16)
+        return mm(hot, table[pl.ds(at_z * 2, 2)].reshape(items // nz, D)).astype(BF16)
+
+    def look_up(at_z, first):
+        def body(t, carry):
+            rows = at(t, step)
+            found = picked_rows(rows, at_z)
+            embedded[rows, :] = found if first else embedded[rows, :] + found
+            return carry
+
+        lax.fori_loop(0, length // step, body, 0)
+
+    def pass_on(n):
+        arrive(cot_half(sides[n][0], n), s_g + 2 * n + n)
+        push(cot_half(sides[n][0], n), cot_half(sides[n][0], n), s_g + 4 + n, sides[1 - n])
+
+    table_over_z(0)
+    table_over_z(1)
+    arrive(table.at[z * 2 + other], s_tc + z * nb)
+    look_up(z, True)
+    table_over_z(2)
+    own_half(0)
+    own_half(1)
+    for n in range(2):
+        for m in range(nz - 1):
+            shard_next(n, m)
+    table_over_blk(0)
+    table_over_blk(1)
+    table_over_core(0)
+    shard_start(2)
+    look_up(near[0], False)
+    table_over_blk(2)
+    table_over_core(1)
+    look_up(near[1], False)
+    pass_on(0)
+    table_over_core(2)
+
+    def shards_over_core(n):
+        for m in (z, *near):
+            arrive(shard_of(n, m * 2 + other), s_wc + n * nz + m)
+
+    shards_over_core(0)
+    shards_over_core(1)
+
+    lane = iota((1, LANES), 1)
     for q in range(nb):
-        total = small[q, 0].astype(F32)
-        for r in range(1, nd):
-            total = total + small[q, r].astype(F32)
+        total = jnp.zeros((16, LANES), F32)
+        for r in range(nd):
+            turned = pltpu.roll(small[r].astype(F32), (r - q) * width % LANES, 1)
+            total = jnp.where(lane // width == r, turned, total)
         small_all[q] = total
     gain_one = jnp.concatenate([small_all[q][0:1] for q in range(nb)], axis=1)
     shift_one = jnp.concatenate([small_all[q][1:2] for q in range(nb)], axis=1)
@@ -493,20 +580,16 @@
     gain_one_own = mine[0:1]
     gain_two, shift_two = mine[2:3], mine[3:4]
     pos_row, time_row = mine[4:5], mine[5:6]
-    lane = iota((1, LANES), 1)
     low = lane < NB
     pos_rows = (0.5 * pltpu.roll(pos_row, NB, 1), 0.5 * pos_row)
     time_rows = (0.5 * time_row, 0.5 * pltpu.roll(time_row, NB, 1))
     masks = (low, lane >= NB)
 
-    step = 256
-
     def embed(t, carry):
         rows = at(t, step)
-        picked = column[rows, 0:1]
-        hot = jnp.where(iota((step, items), 1) == picked, 1.0, 0.0).astype(BF16)
-        found = mm(hot, table[...].reshape(items, D))
-        embedded[rows, :] = found.astype(BF16)
+        found = embedded[rows, :] + picked_rows(rows, near[2])
+        embedded[rows, :] = found
+        found = found.astype(F32)
         mean = jnp.mean(found, axis=1, keepdims=True)
         centered = found - mean
         inverse = lax.rsqrt(jnp.mean(centered * centered, axis=1, keepdims=True) + norm_eps)
@@ -529,10 +612,13 @@
             key[h, rows, LANES:] = jnp.where(low, time_rows[h], pos_hot).astype(BF16)
         return carry
 
-    lax.fori_loop(0, length // step, embed, 0)
+    lax.fori_loop(0, length // step // 2, embed, 0)
+    pass_on(1)
+    for m in range(nz - 1):
+        shard_next(2, m)
+    lax.fori_loop(length // step // 2, length // step, embed, 0)
+    shards_over_core(2)
     out_rows = outw[b].reshape(part, D)
-    for k in range(1, nb):
-        arrive(cot.at[blk_from(k)], s_g + k)
 
     s_st = slots(nb * nb)
     inv_length = 1.0 / length
@@ -559,6 +645,14 @@
         tile(i, True)
         att = jnp.where(low, dq[0, :, 0:LANES], dq[1, :, 0:LANES]) * inv_length
         attended[rows, :] = att
+
+        @pl.when(r == 0)
+        def cotangents():
+            cross = nb - 1 - b
+            for n in range(2):
+                arrive(cot_half(sides[n][0], 1 - n), s_g + 2 * (1 - n) + n)
+                arrive(cot_half(cross, n), s_g + 4 + n)
+
         gg = mm(cot[i], out_rows, NT)
         grad_gated[rows, :] = gg
         g = gg * gate[rows, :] * gain_two
@@ -576,6 +670,10 @@
         return carry
 
     lax.fori_loop(0, nb, forward, 0)
+
+    s_ox = slots(nb)
+    for k in range(1, nb):
+        push(outw.at[b], outw.at[b], s_ox + k, blk_peer(k))
 
     s_ps, s_s1 = slots(nb * nb), slots(nb * nb)
     dk[...] = jnp.zeros(dk.shape, F32)
@@ -784,6 +882,7 @@
 
     for k in range(1, nb):
         arrive(gated_got.at[blk_from(k)], s_gt + k)
+        arrive(outw.at[blk_from(k)], s_ox + k)
     result = embedded[at(b, group), :].astype(F32)
     for q in range(nb):
         result = result + mm(gated_got[q], outw[q].reshape(part, D))
@@ -800,47 +899,27 @@
         push(table_own.at[to[0]], table_got.at[b], s_tgx + k, to)
     table_got[b] = table_own[b]
 
-    grad_out = z_sum(go_z, go_zgot, s_goz)[0]
-    new_m_out[...], new_s_out[...], new_w_out[...] = adam_update(
-        proj_out[...], grad_out, moment_out[...], second_out[...], rate_out
-    )
+    grad_out_out[...] = z_sum(go_z, go_zgot, s_goz)[0]
     totals = little_z[...]
     for k in range(1, nz):
         arrive(little_zgot.at[k], s_lz + k)
         totals = totals + little_zgot[k]
-    little_all[...] = totals
-    shifted = pltpu.roll(little_all[0:8, :], lax.rem(LANES - d * width, LANES), 1)[0:6, 0:width]
-    new_m_small[...], new_s_small[...], new_w_small[...] = adam_update(
-        small_in[...], shifted, moment_small[...], second_small[...], rate_small
-    )
-    per_row = LANES // rows_table
-    count_row = little_all[pl.ds(8 + d // per_row, 1), :]
-    count_row = pltpu.roll(
-        jnp.broadcast_to(count_row, (8, LANES)),
-        lax.rem(LANES - lax.rem(d, per_row) * rows_table, LANES), 1,
-    )[0:1, 0:rows_table]
-    counts_out[...] = count_row
-    logq_out[...] = jnp.log(jnp.maximum(count_row, 1.0) * (1.0 / tokens))
-
+    little_out[...] = totals
     for k in range(1, nb):
         arrive(gi_got.at[blk_from(k)], s_gix + k)
-    grad_in = jnp.concatenate(
-        [gi_got[q][:, s * part : (s + 1) * part] for s in range(4) for q in range(nb)], axis=1
-    )
-    new_m_in[...], new_s_in[...], new_w_in[...] = adam_update(
-        proj_in[...], grad_in, moment_in[...], second_in[...], rate_in
-    )
+    grad_in_out[...] = gi_got[...]
     for k in range(1, nb):
         arrive(ig_got.at[blk_from(k)], s_ig + k)
-    for q in range(nb):
-        input_grad[:, q * part : (q + 1) * part] = ig_got[q].astype(F32)
+    input_out[...] = ig_got[...]
     for k in range(1, nb):
         arrive(table_got.at[blk_from(k)], s_tgx + k)
-    for q in range(nb):
-        table_grad[:, q * part : (q + 1) * part] = table_got[q]
-
-    for args in pending:
-        copy(*args).wait_send()
+    table_out[...] = table_got[...]
+
+    for where, *sent in pending:
+        if where is None:
+            copy(*sent).wait_send()
+        else:
+            pl.when(where)(copy(*sent).wait_send)
 
     def drain(i, carry):
         for k in range(1, nb):
@@ -852,6 +931,48 @@
 
     lax.fori_loop(0, nb, drain, 0)
     assert counter[0] <= send.shape[0], counter[0]
+
+
+def finish_kernel(sizes, *refs):
+    nb, nz, group, items, weight_rows, tokens = sizes
+    part = D // nb
+    rows_table = items // (nb * nz * 2)
+    (
+        layer_in, input_in, table_in, grad_in_in, grad_out_in, little_in,
+        proj_in, proj_out, small_in,
+        moment_in, second_in, moment_out, second_out, moment_small, second_small,
+        layer_out, input_grad, table_grad, counts_out, logq_out,
+        new_m_in, new_s_in, new_w_in, new_m_out, new_s_out, new_w_out,
+        new_m_small, new_s_small, new_w_small,
+    ) = refs
+    d = lax.axis_index("dp")
+    layer_out[...] = layer_in[...]
+    for q in range(nb):
+        cols = slice(q * part, (q + 1) * part)
+        input_grad[:, cols] = input_in[q].astype(F32)
+        table_grad[:, cols] = table_in[q]
+        for s in range(4):
+            own = slice(s * D + q * part, s * D + (q + 1) * part)
+            new_m_in[:, own], new_s_in[:, own], new_w_in[:, own] = adam_update(
+                proj_in[:, own], grad_in_in[q, :, s * part : (s + 1) * part],
+                moment_in[:, own], second_in[:, own], rate_in,
+            )
+    new_m_out[...], new_s_out[...], new_w_out[...] = adam_update(
+        proj_out[...], grad_out_in[...], moment_out[...], second_out[...], rate_out
+    )
+    width = small_in.shape[1]
+    shifted = pltpu.roll(little_in[0:8, :], lax.rem(LANES - d * width, LANES), 1)[0:6, 0:width]
+    new_m_small[...], new_s_small[...], new_w_small[...] = adam_update(
+        small_in[...], shifted, moment_small[...], second_small[...], rate_small
+    )
+    per_row = LANES // rows_table
+    count_row = little_in[pl.ds(8 + d // per_row, 1), :]
+    count_row = pltpu.roll(
+        jnp.broadcast_to(count_row, (8, LANES)),
+        lax.rem(LANES - lax.rem(d, per_row) * rows_table, LANES), 1,
+    )[0:1, 0:rows_table]
+    counts_out[...] = count_row
+    logq_out[...] = jnp.log(jnp.maximum(count_row, 1.0) * (1.0 / tokens))
 
 
 def fused(sizes, args):
@@ -866,6 +987,10 @@
     ) = args
     width = small_params.shape[1]
     shape = jax.ShapeDtypeStruct
+    middle = [
+        shape((group, D), BF16), shape((nb, group, part), BF16), shape((nb, rows_table, part), F32),
+        shape((nb, weight_rows, 4 * part), F32), shape((weight_rows, D), F32), shape((16, LANES), F32),
+    ]
     outs = [
         shape((group, D), BF16), shape((group, D), F32), shape((rows_table, D), F32),
         shape((1, rows_table), F32), shape((1, rows_table), F32),
@@ -882,7 +1007,8 @@
         vm((nb, nd, weight_rows, 4 * part), BF16),
         vm((nb, weight_rows, 4 * part), BF16),
         vm((nb, nd, weight_rows, D), BF16),
-        vm((nb, nd, 16, LANES), BF16),
+        vm((nb, 16, LANES), BF16),
+        vm((nd, 16, LANES), BF16),
         vm((nb, 16, LANES), F32),
         vm((nb, group, D), BF16),
         vm((length, D), BF16),
@@ -927,14 +1053,13 @@
         vm((nz, 1, weight_rows, D), BF16),
         vm((nz, 1, weight_rows, D), BF16),
         vm((16, LANES), F32), vm((16, LANES), F32), vm((16, LANES), F32), vm((nz, 16, LANES), F32),
-        vm((16, LANES), F32),
     ]
     whole, far = pl.BlockSpec(memory_space=pltpu.VMEM), pl.BlockSpec(memory_space=pl.ANY)
-    got = pl.pallas_call(
+    between = pl.pallas_call(
         functools.partial(fused_kernel, sizes),
-        out_shape=outs,
-        in_specs=[whole] * 3 + [far] + [whole] * 3 + [far] + [whole] * 6,
-        out_specs=[whole] * len(outs),
+        out_shape=middle,
+        in_specs=[whole] * 3 + [far] + [whole] * 3 + [far],
+        out_specs=[whole] * len(middle),
         scratch_shapes=scratch,
         compiler_params=pltpu.CompilerParams(
             collective_id=0, has_side_effects=True, vmem_limit_bytes=60 * 2**20
@@ -944,6 +1069,15 @@
         item_ids, pos_buckets, time_buckets,
         item_table.reshape(nb, item_table.shape[0] // nb, D),
         proj_in, proj_out, small_params, out_grad.reshape(group, D),
+    )
+    got = pl.pallas_call(
+        functools.partial(finish_kernel, sizes),
+        out_shape=outs,
+        in_specs=[whole] * (len(middle) + 9),
+        out_specs=[whole] * len(outs),
+        name="hstu_finish",
+    )(
+        *between, proj_in, proj_out, small_params,
         moment_in, second_in, moment_out, second_out, moment_small, second_small,
     )
     return (
@@ -960,7 +1094,7 @@
     by_heads = (
         seq_count == 1 and nd % 2 == 0 and D // nb == LANES and group % 256 == 0
         and items <= 2048 and items // (nb * nd) % 16 == 0 and proj_in.shape[0] % 16 == 0
-        and small_params.shape[1] * nd == LANES
+        and small_params.shape[1] * nd == LANES and nb == 4 and nd == 8
     )
     if by_heads:
         sizes = (nb, nd // 2, group, items, proj_in.shape[0], nd * nb * group)

time: 135 us -> 113 us (0.84)
  local copies, waits for them, and re-layouts: 11.6 us -> 0 us
  Pallas kernels: 122 us -> 113 us
    unnamed x40 -> x0, local copies, waits for them, and re-layouts: 11.6 us -> none
    pallas_call x1 -> x2, Pallas kernels: 122 us -> 113 us  [the longest x1 110 us: fused(): pl.pallas_call(functools.partial(fused_kernel, sizes), out_shape=middle,...]
where the time goes in v2:
time: 113 us
  Pallas kernels  113 us (100%)
    pallas_call x1, Pallas kernels, fused(): pl.pallas_call(functools.partial(fused_kernel, sizes), out_shape=middle,...  110 us
    pallas_call x1, Pallas kernels, fused(): pl.pallas_call(functools.partial(finish_kernel, sizes), out_shape=outs, i...  2.97 us

profile of v2, /device:TPU:0, one launch (start us, length us, event | category | flops | bytes accessed | tf_op | source)
XLA Modules:
  0.0 113.2 jit_solution(14290474759382267751)
XLA Ops:
  0.6 109.6 %hstu_step.1 = (bf16[512,512]{1,0:T(8,128)(2,1)}, bf16[4,512,128]{2,1,0:T(8,128)(2,1)}, f32[4,64,128]{2,1,0:T(8,128)}, f32[4,16,512]{2,1,0:T(8,128)}, f32[16,512]{1,0:T(8,128)}, /*index=5*/f32[16,128]{1,0:T(8,128)}) custom-call(s32[1,512]{1,0:T(1,128)} %refs_0_.1, s32[1,512]{1,0:T(1,128)} %refs_1_.1, s32[1,512]{1,0:T(1,128)} %refs_2_.1, ...), custom_call_target="tpu_custom_call" | custom-call | tf_op jit(solution)/shard_map/hstu_step/pallas_call | solution.py:1058
  110.2 3.0 %hstu_finish.1 = (bf16[512,512]{1,0:T(8,128)(2,1)}, f32[512,512]{1,0:T(8,128)}, f32[64,512]{1,0:T(8,128)}, f32[1,64]{1,0:T(1,128)}, f32[1,64]{1,0:T(1,128)}, /*i...) custom-call(bf16[512,512]{1,0:T(8,128)(2,1)} %get-tuple-element.34.r, ...), custom_call_target="tpu_custom_call" | custom-call | tf_op jit(solution)/shard_map/hstu_finish/pallas_call | solution.py:1073

commit v3 on v2

--- a/solution.py
+++ b/solution.py
@@ -335,18 +335,24 @@
         ids_in, pos_in, time_in, table_in, proj_in, proj_out, small_in, out_grad_in,
         layer_out, input_out, table_out, grad_in_out, grad_out_out, little_out,
         send, recv, local,
-        index, column, padded, table, weight, weight_send, outw, small_send, small, small_all, cot,
+        index, own_index, column, own_column, padded, table, weight, weight_send, outw,
+        small, small_all, cot,
         embedded, normed, projected, gate, value, query, key, attended,
         grad_gated, stats, fix, gated_send, gated_got, grad_att, dq, dk, dv,
-        grad_pre, part_send, part_got, stats_one, ig_send, ig_got, bias_sum, gain_sum,
-        table_sum, table_core, table_z, table_zgot, table_own, table_got,
-        gi_sum, gi_core, gi_z, gi_zgot, gi_own, gi_got,
-        go_sum, go_core, go_z, go_zgot, little, little_core, little_z, little_zgot,
+        grad_pre, part_send, part_core, part_x, part_got, stats_one, ig_send, ig_got,
+        bias_sum, gain_sum, table_acc,
+        table_sum, table_core, table_z, table_got,
+        gi_sum, gi_core, gi_z, gi_got,
+        go_sum, go_core, go_z, go_got,
+        little, little_parts, little_all, little_got,
     ) = refs
     b = lax.axis_index("blk")
     d = lax.axis_index("dp")
-    z, core = d // 2, d % 2
-    other = 1 - core
+    y, x, z, core = b // 2, b % 2, d // 2, d % 2
+    other, off_y, off_x = 1 - core, 1 - y, 1 - x
+    v = core * 2 + x
+    home = core == y
+    away = core != y
 
     counter = [0]
 
@@ -378,6 +384,15 @@
         return (b, z_to(k) * 2 + core)
 
     core_peer = (b, z * 2 + other)
+    x_peer, y_peer = (y * 2 + off_x, d), (off_y * 2 + x, d)
+    partner = (off_y * 2 + x, z * 2 + other)
+
+    def row_peer(k):
+        w = lax.rem(v + k, nb)
+        return w, (y * 2 + w % 2, z * 2 + w // 2)
+
+    def row_from(k):
+        return lax.rem(v + nb - k, nb)
 
     pending = []
 
@@ -392,98 +407,116 @@
         pending.append((where, src, dst, slot, target))
 
     near = (z + 1 - 2 * (z % 2), 2 - z // 2, 3 * (1 - z // 2))
-
-    def chain_start(ref, base):
-        for n, (beside, there) in enumerate(((z - 1, z > 0), (z + 1, z < nz - 1))):
-            to = jnp.clip(beside, 0, nz - 1)
-            push(ref, ref, base + n, (b, to * 2 + core), base + z, there)
-
-    def chain_next(ref, base, n):
-        arrive(ref, base + near[n])
-        beyond = jnp.where(near[n] < z, z + 1, z - 1)
-        there = jnp.logical_and(beyond >= 0, beyond < nz)
-        to = jnp.clip(beyond, 0, nz - 1)
-        push(ref, ref, base + 2 + n, (b, to * 2 + core), base + near[n], there)
-
-    def arrive(dst, slot):
-        copy(dst, dst, slot, core_peer).wait_recv()
+    steps = [(kr, kz) for kz in range(nz) for kr in range(nb) if kr + kz > 0]
+
+    def slab(kr, kz):
+        w, at_z = lax.rem(v + kr, nb), z_to(kz)
+        return w, at_z, (y * 2 + w % 2, at_z * 2 + w // 2)
+
+    def slab_from(kr, kz):
+        return row_from(kr), z_from(kz)
+
+    def arrive(dst, slot, where=None):
+        wait = copy(dst, dst, slot, core_peer).wait_recv
+        if where is None:
+            wait()
+        else:
+            pl.when(where)(wait)
 
     table_load = pltpu.make_async_copy(table_in, table.at[d], local.at[0])
     table_load.start()
     cot_load = pltpu.make_async_copy(out_grad_in, cot.at[b], local.at[1])
-    cot_load.start()
-
-    index[b] = jnp.concatenate(
+    pl.when(home)(cot_load.start)
+    own_index[...] = jnp.concatenate(
         [ids_in[...], pos_in[...], time_in[...], jnp.zeros((5, group), I32)], axis=0
     )
+
+    @pl.when(home)
+    def keep_index():
+        index[b] = own_index[...]
+
     own_rows = proj_in[...].astype(BF16)
     for q in range(nb):
         weight_send[q] = jnp.concatenate(
             [own_rows[:, s * D + q * part : s * D + (q + 1) * part] for s in range(4)], axis=1
         )
-    weight[b, d] = weight_send[b]
+    weight[y, x, z, core] = weight_send[v]
     outw[b, d] = proj_out[...].astype(BF16)
     width = small_in.shape[1]
-    spread = (iota((width, LANES), 1) == iota((width, LANES), 0) + b * width).astype(F32)
+    spread = (iota((width, LANES), 1) == iota((width, LANES), 0) + d * width).astype(F32)
     small_pad = jnp.concatenate([small_in[...], jnp.zeros((10, width), F32)], axis=0)
-    small_send[b] = mm(small_pad.astype(BF16), spread.astype(BF16)).astype(BF16)
+    small[y, x, z, core] = mm(small_pad.astype(BF16), spread.astype(BF16)).astype(BF16)
 
     barrier = pltpu.get_barrier_semaphore()
-    peers = [blk_peer(k) for k in range(1, nb)] + [z_peer(k) for k in range(1, nz)] + [core_peer]
+    peers = [slab(*k)[2] for k in steps]
+    peers += [(off_y * 2 + x, z_to(kz) * 2 + c) for kz in range(nz) for c in range(2)]
+    peers += [(off_y * 2 + off_x, z * 2 + c) for c in range(2)]
     for target in peers:
         pl.semaphore_signal(
             barrier, inc=1, device_id={"blk": target[0], "dp": target[1]}, device_id_type=MESH
         )
     pl.semaphore_wait(barrier, len(peers))
 
-    s_index, s_w, s_s = slots(nb), slots(nb), slots(nb)
-    for k in range(1, nb):
-        to = blk_peer(k)
-        push(index.at[b], index.at[b], s_index + k, to)
-        push(weight_send.at[to[0]], weight.at[b, d], s_w + k, to)
-        push(small_send.at[b], small_send.at[b], s_s + k, to)
     table_load.wait()
-    s_tz, s_tx, s_tc = slots(nz + 2), slots(nz * nb), slots(nz * nb)
-    chain_start(table.at[d, b], s_tz)
+    s_tz, s_tx, s_tc = slots(nz), slots(nz * nb), slots(nz * nb)
+    for n in range(nz - 1):
+        push(table.at[d, b], table.at[d, b], s_tz + n, (b, near[n] * 2 + core), s_tz + z)
     push(table.at[d], table.at[d], s_tc, core_peer, s_tc + z * nb)
-    cot_load.wait()
-    s_g = slots(6)
-    x_peer, y_peer = (b // 2 * 2 + 1 - b % 2, d), (lax.rem(b + 2, nb), d)
+    s_index, s_w, s_s = slots(nb), slots(nb * nz), slots(nb * nz)
+    for k in range(nb):
+        to = (core * 2 + (x + k % 2) % 2, z * 2 + (core + k // 2) % 2)
+        push(own_index, index.at[b], s_index + k, to, s_index + b, away if k == 0 else None)
+    for kr, kz in steps:
+        w, at_z, to = slab(kr, kz)
+        push(weight_send.at[w], weight.at[y, x, z, core], s_w + kz * nb + kr, to)
+    for kr, kz in steps:
+        w, at_z, to = slab(kr, kz)
+        push(small.at[y, x, z, core], small.at[y, x, z, core], s_s + kz * nb + kr, to)
+    s_g = slots(8)
     halves = (slice(0, group // 2), slice(group // 2, group))
-    sides = (x_peer, y_peer)
+    v_x, v_core, v_cross = core * 2 + off_x, other * 2 + x, other * 2 + off_x
 
     def cot_half(owner, n):
         return cot.at[owner, halves[n]]
 
-    def own_half(n):
-        for m in range(2):
-            push(cot_half(b, n), cot_half(b, n), s_g + 2 * n + m, sides[m])
-
-    s_wz, s_wc = slots(3 * (nz + 2)), slots(3 * nz)
-
-    def shard_of(n, slot):
-        return (weight.at[:, slot], small.at[slot], outw.at[b, slot])[n]
-
-    def shard_start(n):
-        for k in range(1, nz):
-            push(shard_of(n, d), shard_of(n, d), s_wz + n * (nz + 2) + k, z_peer(k), s_wz + n * (nz + 2) + z)
-        push(shard_of(n, d), shard_of(n, d), s_wc + n * nz, core_peer, s_wc + n * nz + z)
-
-    def shard_next(n, m):
-        ref = shard_of(n, near[m] * 2 + core)
-        arrive(ref, s_wz + n * (nz + 2) + near[m])
-        push(ref, ref, s_wc + n * nz + 1 + m, core_peer, s_wc + n * nz + near[m])
-
-    for k in range(1, nb):
-        arrive(weight.at[blk_from(k), d], s_w + k)
-    shard_start(0)
-    for k in range(1, nb):
-        arrive(small_send.at[blk_from(k)], s_s + k)
-    small[d] = sum(small_send[q].astype(F32) for q in range(nb)).astype(BF16)
-    shard_start(1)
-
-    for k in range(1, nb):
-        arrive(index.at[blk_from(k)], s_index + k)
+    def cross_over():
+        for n in range(2):
+            push(out_grad_in.at[halves[n]], cot_half(b, n), s_g + n, partner, None, away)
+        pl.when(home)(cot_load.wait)
+
+    def own_half(n, where):
+        push(cot_half(v, n), cot_half(v, n), s_g + 2 + n, x_peer, None, where)
+        push(cot_half(v, n), cot_half(v, n), s_g + 4 + n, core_peer, None, where)
+
+    def pass_on(n):
+        arrive(cot_half(v_x, n), s_g + 2 + n)
+        push(cot_half(v_x, n), cot_half(v_x, n), s_g + 6 + n, core_peer)
+
+    s_wc, s_oz = slots(3 * nz), slots(nz)
+    sides, opposite, second = (y, y, core), (off_y, off_y, other), (y_peer, y_peer, core_peer)
+
+    def shard_of(n, side, at_z):
+        if n == 2:
+            return outw.at[b, at_z * 2 + side]
+        return (weight, small)[n].at[side, :, at_z]
+
+    def shard_next(n, kz):
+        at_z = z_from(kz)
+        if n == 2 and kz > 0:
+            arrive(outw.at[b, at_z * 2 + core], s_oz + kz)
+        for kr in range(nb):
+            if n < 2 and kr + kz > 0:
+                w = row_from(kr)
+                arrive((weight, small)[n].at[y, w % 2, at_z, w // 2], (s_w, s_s)[n] + kz * nb + kr)
+        ref = shard_of(n, sides[n], at_z)
+        push(ref, ref, s_wc + n * nz + kz, second[n])
+
+    def shards_end(n):
+        for kz in range(nz):
+            arrive(shard_of(n, opposite[n], z_from(kz)), s_wc + n * nz + kz)
+
+    for i in range(nb):
+        arrive(index.at[i], s_index + i, jnp.logical_or(away, b != i))
     padded[...] = jnp.zeros(padded.shape, F32)
 
     def to_column(e, carry):
@@ -492,12 +525,14 @@
         return carry
 
     lax.fori_loop(0, nb, to_column, 0)
+    padded[0:8, :] = own_index[...].astype(F32)
+    own_column[...] = jnp.transpose(padded[...]).astype(I32)
 
     step = 256
 
     def table_over_z(n):
         shard = near[n] * 2 + core
-        chain_next(table.at[shard, b], s_tz, n)
+        arrive(table.at[shard, b], s_tz + near[n])
         for m in range(1, nb):
             push(
                 table.at[shard, b], table.at[shard, b], s_tx + n * nb + m, blk_peer(m),
@@ -521,62 +556,56 @@
         for m in range(1, nb):
             arrive(table.at[shard, blk_from(m)], s_tc + near[n] * nb + m)
 
-    def picked_rows(rows, at_z):
+    def picked_rows(rows, at_z, step=step):
         picked = column[rows, 0:1] - at_z * (items // nz)
         hot = jnp.where(iota((step, items // nz), 1) == picked, 1.0, 0.0).astype(BF16)
         return mm(hot, table[pl.ds(at_z * 2, 2)].reshape(items // nz, D)).astype(BF16)
 
     def look_up(at_z, first):
         def body(t, carry):
-            rows = at(t, step)
-            found = picked_rows(rows, at_z)
+            rows = at(t, group)
+            found = picked_rows(rows, at_z, group)
             embedded[rows, :] = found if first else embedded[rows, :] + found
             return carry
 
-        lax.fori_loop(0, length // step, body, 0)
-
-    def pass_on(n):
-        arrive(cot_half(sides[n][0], n), s_g + 2 * n + n)
-        push(cot_half(sides[n][0], n), cot_half(sides[n][0], n), s_g + 4 + n, sides[1 - n])
+        lax.fori_loop(0, nb, body, 0)
 
     table_over_z(0)
     table_over_z(1)
     arrive(table.at[z * 2 + other], s_tc + z * nb)
     look_up(z, True)
     table_over_z(2)
-    own_half(0)
-    own_half(1)
-    for n in range(2):
-        for m in range(nz - 1):
-            shard_next(n, m)
+    for k in range(1, nz):
+        push(outw.at[b, d], outw.at[b, d], s_oz + k, z_peer(k))
+    shard_next(0, 0)
+    shard_next(0, 1)
     table_over_blk(0)
     table_over_blk(1)
+    shard_next(0, 3)
+    shard_next(0, 2)
+    for kz in range(nz):
+        shard_next(1, kz)
+    cross_over()
     table_over_core(0)
-    shard_start(2)
     look_up(near[0], False)
+    own_half(0, home)
+    own_half(1, home)
     table_over_blk(2)
     table_over_core(1)
     look_up(near[1], False)
-    pass_on(0)
+    for kz in range(nz):
+        shard_next(2, kz)
     table_over_core(2)
-
-    def shards_over_core(n):
-        for m in (z, *near):
-            arrive(shard_of(n, m * 2 + other), s_wc + n * nz + m)
-
-    shards_over_core(0)
-    shards_over_core(1)
+    shards_end(0)
+    shards_end(1)
 
     lane = iota((1, LANES), 1)
     for q in range(nb):
-        total = jnp.zeros((16, LANES), F32)
-        for r in range(nd):
-            turned = pltpu.roll(small[r].astype(F32), (r - q) * width % LANES, 1)
-            total = jnp.where(lane // width == r, turned, total)
+        total = sum(small[q // 2, q % 2, r // 2, r % 2].astype(F32) for r in range(nd))
         small_all[q] = total
     gain_one = jnp.concatenate([small_all[q][0:1] for q in range(nb)], axis=1)
     shift_one = jnp.concatenate([small_all[q][1:2] for q in range(nb)], axis=1)
-    mine = small_all[b]
+    mine = small_all[v]
     gain_one_own = mine[0:1]
     gain_two, shift_two = mine[2:3], mine[3:4]
     pos_row, time_row = mine[4:5], mine[5:6]
@@ -613,12 +642,13 @@
         return carry
 
     lax.fori_loop(0, length // step // 2, embed, 0)
-    pass_on(1)
-    for m in range(nz - 1):
-        shard_next(2, m)
+    shards_end(2)
+    s_oy, s_ox = slots(1), slots(2)
+    push(outw.at[b], outw.at[b], s_oy, y_peer)
+    for n in range(2):
+        arrive(cot_half(v, n), s_g + n, away)
+        own_half(n, away)
     lax.fori_loop(length // step // 2, length // step, embed, 0)
-    shards_over_core(2)
-    out_rows = outw[b].reshape(part, D)
 
     s_st = slots(nb * nb)
     inv_length = 1.0 / length
@@ -646,13 +676,24 @@
         att = jnp.where(low, dq[0, :, 0:LANES], dq[1, :, 0:LANES]) * inv_length
         attended[rows, :] = att
 
-        @pl.when(r == 0)
+        @pl.when(r == 1)
         def cotangents():
-            cross = nb - 1 - b
-            for n in range(2):
-                arrive(cot_half(sides[n][0], 1 - n), s_g + 2 * (1 - n) + n)
-                arrive(cot_half(cross, n), s_g + 4 + n)
-
+            pass_on(0)
+            pass_on(1)
+
+        return carry
+
+    lax.fori_loop(0, nb, forward, 0)
+    arrive(outw.at[off_y * 2 + x], s_oy)
+    out_rows = outw[v].reshape(part, D)
+    for n in range(2):
+        arrive(cot_half(v_core, n), s_g + 4 + n)
+        arrive(cot_half(v_cross, n), s_g + 6 + n)
+
+    def statistics(r, carry):
+        i = nb - 1 - r
+        rows = at(i, group)
+        att = attended[rows, :]
         gg = mm(cot[i], out_rows, NT)
         grad_gated[rows, :] = gg
         g = gg * gate[rows, :] * gain_two
@@ -664,18 +705,19 @@
         packed = jnp.where(
             lane == 0, mean, jnp.where(lane == 1, square, jnp.where(lane == 2, sum_g, sum_ga))
         )
-        stats[b, i] = jnp.transpose(packed)[0:8]
+        packed = jnp.transpose(packed)
+        stats[v, i] = jnp.concatenate(
+            [packed[0:4, 0 : group // 2], packed[0:4, group // 2 :]], axis=0
+        )
         for k in range(1, nb):
-            copy(stats.at[b, i], stats.at[b, i], s_st + i * nb + k, blk_peer(k)).start()
+            copy(stats.at[v, i], stats.at[v, i], s_st + i * nb + k, row_peer(k)[1]).start()
         return carry
 
-    lax.fori_loop(0, nb, forward, 0)
-
-    s_ox = slots(nb)
-    for k in range(1, nb):
-        push(outw.at[b], outw.at[b], s_ox + k, blk_peer(k))
-
-    s_ps, s_s1 = slots(nb * nb), slots(nb * nb)
+    lax.fori_loop(0, nb, statistics, 0)
+
+    push(outw.at[v], outw.at[v], s_ox, x_peer)
+
+    s_pc, s_px, s_s1, s_gt = slots(nb), slots(nb), slots(nb * nb), slots(nb)
     dk[...] = jnp.zeros(dk.shape, F32)
     dv[...] = jnp.zeros(dv.shape, F32)
     bias_sum[...] = jnp.zeros(bias_sum.shape, F32)
@@ -685,8 +727,8 @@
         i = nb - 1 - r
         rows = at(i, group)
         for k in range(1, nb):
-            arrive(stats.at[blk_from(k), i], s_st + i * nb + k)
-        every = [stats[q, i] for q in range(nb)]
+            arrive(stats.at[row_from(k), i], s_st + i * nb + k)
+        every = [jnp.concatenate([stats[q, i, 0:4], stats[q, i, 4:8]], axis=1) for q in range(nb)]
         mean = sum(s[0:1] for s in every) * (1.0 / nb)
         square = sum(s[1:2] + part * (s[0:1] - mean) * (s[0:1] - mean) for s in every)
         inverse = lax.rsqrt(square * (1.0 / D) + norm_eps)
@@ -701,6 +743,15 @@
         hat = (attended[rows, :] - turned[:, 0:1]) * inverse
         normal = hat * gain_two + shift_two
         gated_send[i] = (normal * gate[rows, :]).astype(BF16)
+
+        @pl.when(jnp.logical_or(away, i != b))
+        def send_gated():
+            copy(gated_send.at[i], gated_got.at[v], s_gt + i, (i, z * 2 + y), s_gt + v).start()
+
+        @pl.when(jnp.logical_and(home, i == b))
+        def keep_gated():
+            gated_got[v] = gated_send[i]
+
         gg = grad_gated[rows, :]
         grad_u = gg * normal
         grad_norm = gg * gate[rows, :]
@@ -754,74 +805,119 @@
         mean_one, inverse_one = fix[rows, 0:1], fix[rows, 1:2]
         hat_one = (embedded[rows, :].astype(F32) - mean_one) * inverse_one
         second = jnp.sum(scaled * hat_one, axis=1, keepdims=True)
-        stats_one[b, i] = jnp.transpose(jnp.where(lane == 0, first, second))[0:8]
+        turned = jnp.transpose(jnp.where(lane == 0, first, second))
+        stats_one[v, i] = jnp.concatenate(
+            [turned[n : n + 1, at_lane : at_lane + LANES] for n in range(2) for at_lane in range(0, group, LANES)],
+            axis=0,
+        )
         for q in range(nb):
-            part_send[q, i] = partial[:, q * part : (q + 1) * part].astype(BF16)
+            part_send[i, q] = partial[:, q * part : (q + 1) * part].astype(BF16)
+        core_part(i).start()
         for k in range(1, nb):
-            to = blk_peer(k)
-            copy(part_send.at[to[0], i], part_got.at[b, i], s_ps + i * nb + k, to).start()
-            copy(stats_one.at[b, i], stats_one.at[b, i], s_s1 + i * nb + k, to).start()
-        part_got[b, i] = part_send[b, i]
+            copy(stats_one.at[v, i], stats_one.at[v, i], s_s1 + i * nb + k, row_peer(k)[1]).start()
+
+        @pl.when(r > 0)
+        def previous():
+            over_x(i + 1)
+
         return carry
 
+    def core_part(i):
+        half = part_send.at[i, pl.ds(other * 2, 2)]
+        return copy(half, part_core.at[i], s_pc + i, core_peer)
+
+    def x_part(i):
+        return copy(part_x.at[i], part_got.at[i], s_px + i, x_peer)
+
+    def over_x(i):
+        core_part(i).wait_recv()
+        both = part_send[i, v_x].astype(F32) + part_core[i, off_x].astype(F32)
+        part_x[i] = both.astype(BF16)
+        x_part(i).start()
+
     lax.fori_loop(0, nb, backward, 0)
-
-    s_gt = slots(nb)
-    for k in range(1, nb):
-        to = blk_peer(k)
-        push(gated_send.at[to[0]], gated_got.at[b], s_gt + k, to)
-    gated_got[b] = gated_send[b]
-
-    def core_stage(total, landing, base):
-        for k in range(nz):
-            push(total.at[:, k * 2 + other], landing.at[k], base + k, core_peer)
-
-    def core_sum(total, landing, outgoing, base):
-        for k in range(nz):
-            arrive(landing.at[k], base + k)
-            outgoing[k] = (total[:, k * 2 + core].astype(F32) + landing[k].astype(F32)).astype(BF16)
-
-    def z_stage(outgoing, landing, base):
-        for k in range(1, nz):
-            push(outgoing.at[z_to(k)], landing.at[k], base + k, z_peer(k))
-
-    def z_sum(outgoing, landing, base):
-        total = outgoing[z].astype(F32)
-        for k in range(1, nz):
-            arrive(landing.at[k], base + k)
-            total = total + landing[k].astype(F32)
-        return total
-
-    s_gic, s_giz, s_gix = slots(nz), slots(nz), slots(nb)
+    over_x(0)
+    arrive(outw.at[v_x], s_ox)
+    push(outw.at[v_x], outw.at[v_x], s_ox + 1, core_peer)
+
+    def gi_half(side, k):
+        return gi_sum.at[side, :, k]
+
+    def table_half(side, k):
+        return table_sum.at[side, :, k]
+
+    def go_half(side, k):
+        return go_sum.at[k, side]
+
+    order = (near[2], near[1], near[0], z)
+
+    def y_stage(half, landing, base):
+        for n, k in enumerate(order):
+            push(half(off_y, k), landing.at[k], base + n, y_peer)
+
+    def y_sum(half, landing, outgoing, base, n):
+        k = order[n]
+        arrive(landing.at[k], base + n)
+        outgoing[k] = (half(y, k)[...].astype(F32) + landing[k].astype(F32)).astype(BF16)
+
+    def owner_stage(outgoing, landing, base, n):
+        k = order[n]
+        for w in range(nb):
+            to = (y * 2 + w % 2, k * 2 + w // 2)
+            own = n == nz - 1
+            push(
+                outgoing.at[k, w % 2, w // 2], landing.at[v, z], base + n * nb + w, to,
+                base + z * nb + v, v != w if own else None,
+            )
+        if own:
+            landing[v, z] = outgoing[z, x, core]
+
+    def owner_sum(landing, base, result):
+        for n, k in enumerate(order):
+            for w in range(nb):
+                arrive(landing.at[w, k], base + k * nb + w, v != w if n == nz - 1 else None)
+        for q in range(nb):
+            result[q] = sum(landing[q, k].astype(F32) for k in range(nz))
+
+    s_gic, s_gio = slots(nz), slots(nz * nb)
     s_goc, s_goz = slots(nz), slots(nz)
 
     gated_all = gated_send[...].reshape(length, part)
     go_sum[...] = mm(gated_all, cot[...].reshape(length, D), TN).astype(BF16).reshape(go_sum.shape)
-    core_stage(go_sum, go_core, s_goc)
+    y_stage(go_half, go_core, s_goc)
 
     def weight_grad(t, carry):
         cols = at(t, LANES)
         got = mm(normed[:, cols], grad_pre[...], TN).astype(BF16)
-        gi_sum[t] = got.reshape(gi_sum.shape[1:])
+        gi_sum[t // 2, t % 2] = got.reshape(gi_sum.shape[2:])
         return carry
 
     lax.fori_loop(0, nb, weight_grad, 0)
-    core_stage(gi_sum, gi_core, s_gic)
+    y_stage(gi_half, gi_core, s_gic)
 
     s_ig = slots(nb)
 
     def input_part(r, carry):
         i = nb - 1 - r
         rows = at(i, group)
+        x_part(i).wait_recv()
         for k in range(1, nb):
-            arrive(part_got.at[blk_from(k), i], s_ps + i * nb + k)
-            arrive(stats_one.at[blk_from(k), i], s_s1 + i * nb + k)
-        total = sum(part_got[q, i].astype(F32) for q in range(nb))
+            arrive(stats_one.at[row_from(k), i], s_s1 + i * nb + k)
+        total = (
+            part_send[i, v].astype(F32) + part_core[i, x].astype(F32) + part_got[i].astype(F32)
+        )
         row = sum(stats_one[q, i] for q in range(nb)) * (1.0 / D)
-        padded[0:8, :] = row
+        row = jnp.concatenate(
+            [
+                jnp.concatenate([row[n * 4 + m : n * 4 + m + 1] for m in range(4)], axis=1)
+                for n in range(2)
+            ],
+            axis=0,
+        )
+        padded[0:2, :] = row
         turned = jnp.transpose(padded[...])
         mean_one, inverse_one = fix[rows, 0:1], fix[rows, 1:2]
-        mycols = at(b, part)
+        mycols = at(v, part)
         hat_one = (embedded[rows, mycols].astype(F32) - mean_one) * inverse_one
         gain_sum[0:1, :] += jnp.sum(total * hat_one, axis=0, keepdims=True)
         gain_sum[1:2, :] += jnp.sum(total, axis=0, keepdims=True)
@@ -829,32 +925,67 @@
         ig_send[i] = (cot[i, :, mycols].astype(F32) + back).astype(BF16)
         return carry
 
-    lax.fori_loop(0, nb, input_part, 0)
-    for k in range(1, nb):
-        to = blk_peer(k)
-        push(ig_send.at[to[0]], ig_got.at[b], s_ig + k, to)
-    ig_got[b] = ig_send[b]
-
-    s_tgc, s_tgz, s_tgx = slots(nz), slots(nz), slots(nb)
+    s_tgc, s_tgo = slots(nz), slots(nz * nb)
+
+    def gi_over(n):
+        y_sum(gi_half, gi_core, gi_z, s_gic, n)
+        owner_stage(gi_z, gi_got, s_gio, n)
+
+    def table_rows(i, t):
+        hot = jnp.where(iota((group, group), 0) + t * group == index[i][0:1], 1.0, 0.0)
+        return mm(hot.astype(BF16), ig_send[i])
+
+    def table_add(i, first):
+        def add(t, carry):
+            rows = at(t, group)
+            got = table_rows(i, t)
+            table_acc[rows, :] = got if first else table_acc[rows, :] + got
+            return carry
+
+        lax.fori_loop(0, items // group, add, 0)
 
     def table_part(t, carry):
-        picked = jnp.concatenate([index[e][0:1] for e in range(nb)], axis=1)
-        hot = jnp.where(iota((step, length), 0) + t * step == picked, 1.0, 0.0).astype(BF16)
-        got = mm(hot, ig_send[...].reshape(length, part)).astype(BF16)
-        table_sum[t // (items // nb // step), at(t % (items // nb // step), step // rows_table)] = (
-            got.reshape(step // rows_table, rows_table, part)
-        )
+        got = (table_acc[at(t, group), :] + table_rows(0, t)).astype(BF16)
+        table_sum[t // 2, t % 2] = got.reshape(table_sum.shape[2:])
         return carry
 
-    lax.fori_loop(0, items // step, table_part, 0)
-    core_stage(table_sum, table_core, s_tgc)
-
-    s_lc, s_lz = slots(1), slots(nz)
+    for r in range(nb - 1):
+        input_part(r, 0)
+        table_add(nb - 1 - r, r == 0)
+        if r == 1:
+            gi_over(0)
+            gi_over(1)
+        if r == 2:
+            gi_over(2)
+    input_part(nb - 1, 0)
+    lax.fori_loop(off_y * 2, off_y * 2 + 2, table_part, 0)
+    y_stage(table_half, table_core, s_tgc)
+    for k in range(nb):
+        i = lax.rem(b + k, nb)
+        push(ig_send.at[i], ig_got.at[v], s_ig + k, (i, z * 2 + y), s_ig + v, away if k == 0 else None)
+
+    @pl.when(home)
+    def keep_input():
+        ig_got[v] = ig_send[b]
+
+    lax.fori_loop(y * 2, y * 2 + 2, table_part, 0)
+    gi_over(3)
+    for n in range(nz):
+        y_sum(go_half, go_core, go_z, s_goc, n)
+    for k in range(nz):
+        push(go_z.at[z_to(k)], go_got.at[z], s_goz + k, (v, z_to(k) * 2 + y), None, away if k == 0 else None)
+
+    @pl.when(home)
+    def keep_rows():
+        go_got[z] = go_z[z]
+
+
+    s_l, s_lx = slots(nd), slots(1)
     own_items = items // nb
 
     def count(t, carry):
         picked = column[at(t, step), 0:1]
-        hit = jnp.where(iota((step, own_items), 1) + b * own_items == picked, 1.0, 0.0)
+        hit = jnp.where(iota((step, own_items), 1) + v * own_items == picked, 1.0, 0.0)
         return carry + jnp.sum(hit, axis=0, keepdims=True)
 
     counted = lax.fori_loop(0, length // step, count, jnp.zeros((1, own_items), F32))
@@ -867,53 +998,55 @@
     little[5:6, :] = time_grad * halved
     for q in range(own_items // LANES):
         little[8 + q : 9 + q, :] = counted[:, q * LANES : (q + 1) * LANES]
-    push(little, little_core, s_lc, core_peer)
-
-    core_sum(go_sum, go_core, go_z, s_goc)
-    z_stage(go_z, go_zgot, s_goz)
-    core_sum(gi_sum, gi_core, gi_z, s_gic)
-    z_stage(gi_z, gi_zgot, s_giz)
-    arrive(little_core, s_lc)
-    little_z[...] = little[...] + little_core[...]
-    for k in range(1, nz):
-        push(little_z, little_zgot.at[k], s_lz + k, z_peer(k))
-    core_sum(table_sum, table_core, table_z, s_tgc)
-    z_stage(table_z, table_zgot, s_tgz)
-
-    for k in range(1, nb):
-        arrive(gated_got.at[blk_from(k)], s_gt + k)
-        arrive(outw.at[blk_from(k)], s_ox + k)
-    result = embedded[at(b, group), :].astype(F32)
-    for q in range(nb):
-        result = result + mm(gated_got[q], outw[q].reshape(part, D))
-    layer_out[...] = result.astype(BF16)
-
-    gi_own[...] = z_sum(gi_z, gi_zgot, s_giz)
-    for k in range(1, nb):
-        to = blk_peer(k)
-        push(gi_own.at[to[0]], gi_got.at[b], s_gix + k, to)
-    gi_got[b] = gi_own[b]
-    table_own[...] = z_sum(table_z, table_zgot, s_tgz)
-    for k in range(1, nb):
-        to = blk_peer(k)
-        push(table_own.at[to[0]], table_got.at[b], s_tgx + k, to)
-    table_got[b] = table_own[b]
-
-    grad_out_out[...] = z_sum(go_z, go_zgot, s_goz)[0]
-    totals = little_z[...]
-    for k in range(1, nz):
-        arrive(little_zgot.at[k], s_lz + k)
-        totals = totals + little_zgot[k]
-    little_out[...] = totals
-    for k in range(1, nb):
-        arrive(gi_got.at[blk_from(k)], s_gix + k)
-    grad_in_out[...] = gi_got[...]
-    for k in range(1, nb):
-        arrive(ig_got.at[blk_from(k)], s_ig + k)
+    columns = [(ky, kz) for kz in range(nz) for ky in range(2) if ky + kz > 0]
+    for ky, kz in columns:
+        to = (lax.rem(y + ky, 2) * 2 + x, z_to(kz) * 2 + core)
+        push(little, little_parts.at[kz * 2 + ky], s_l + kz * 2 + ky, to)
+    def from_row(landing, base):
+        for w in range(nb):
+            arrive(landing.at[w], base + w, jnp.logical_or(away, v != w))
+
+    from_row(gated_got, s_gt)
+    arrive(outw.at[other * 2 + off_x], s_ox + 1)
+
+    def finish_layer(t, carry):
+        rows = at(t, step)
+        hot = jnp.where(iota((step, items), 1) == own_column[rows, 0:1], 1.0, 0.0).astype(BF16)
+        result = mm(hot, table[...].reshape(items, D))
+        for q in range(nb):
+            result = result + mm(gated_got[q, rows, :], outw[q].reshape(part, D))
+        layer_out[rows, :] = result.astype(BF16)
+        return carry
+
+    lax.fori_loop(0, group // step, finish_layer, 0)
+
+    for n in range(nz):
+        y_sum(table_half, table_core, table_z, s_tgc, n)
+        owner_stage(table_z, table_got, s_tgo, n)
+    totals = little[...]
+    for ky, kz in columns:
+        arrive(little_parts.at[kz * 2 + ky], s_l + kz * 2 + ky)
+        totals = totals + little_parts[kz * 2 + ky]
+    little_all[...] = totals
+    push(little_all, little_got, s_lx, core_peer)
+
+    owner_sum(gi_got, s_gio, grad_in_out)
+    for k in range(nz):
+        arrive(go_got.at[z_from(k)], s_goz + k, away if k == 0 else None)
+    grad_out_out[...] = sum(go_got[k].astype(F32) for k in range(nz))
+    from_row(ig_got, s_ig)
     input_out[...] = ig_got[...]
-    for k in range(1, nb):
-        arrive(table_got.at[blk_from(k)], s_tgx + k)
-    table_out[...] = table_got[...]
+    arrive(little_got, s_lx)
+
+    @pl.when(home)
+    def keep_own():
+        little_out[...] = little_all[...]
+
+    @pl.when(away)
+    def take_peers():
+        little_out[...] = little_got[...]
+
+    owner_sum(table_got, s_tgo, table_out)
 
     for where, *sent in pending:
         if where is None:
@@ -923,10 +1056,13 @@
 
     def drain(i, carry):
         for k in range(1, nb):
-            to = blk_peer(k)
-            copy(stats.at[b, i], stats.at[b, i], s_st + i * nb + k, to).wait_send()
-            copy(part_send.at[to[0], i], part_got.at[b, i], s_ps + i * nb + k, to).wait_send()
-            copy(stats_one.at[b, i], stats_one.at[b, i], s_s1 + i * nb + k, to).wait_send()
+            to = row_peer(k)[1]
+            copy(stats.at[v, i], stats.at[v, i], s_st + i * nb + k, to).wait_send()
+            copy(stats_one.at[v, i], stats_one.at[v, i], s_s1 + i * nb + k, to).wait_send()
+        core_part(i).wait_send()
+        x_part(i).wait_send()
+        sent_gated = copy(gated_send.at[i], gated_got.at[v], s_gt + i, (i, z * 2 + y), s_gt + v)
+        pl.when(jnp.logical_or(away, i != b))(sent_gated.wait_send)
         return carry
 
     lax.fori_loop(0, nb, drain, 0)
@@ -999,16 +1135,17 @@
     ]
     vm = pltpu.VMEM
     scratch = [
-        pltpu.SemaphoreType.DMA((192,)), pltpu.SemaphoreType.DMA((192,)), pltpu.SemaphoreType.DMA((2,)),
+        pltpu.SemaphoreType.DMA((256,)), pltpu.SemaphoreType.DMA((256,)), pltpu.SemaphoreType.DMA((2,)),
         vm((nb, 8, group), I32),
+        vm((8, group), I32),
         vm((length, LANES), I32),
+        vm((group, LANES), I32),
         vm((LANES, group), F32),
         vm((nd, nb, rows_table, D), BF16),
-        vm((nb, nd, weight_rows, 4 * part), BF16),
+        vm((2, 2, nz, 2, weight_rows, 4 * part), BF16),
         vm((nb, weight_rows, 4 * part), BF16),
         vm((nb, nd, weight_rows, D), BF16),
-        vm((nb, 16, LANES), BF16),
-        vm((nd, 16, LANES), BF16),
+        vm((2, 2, nz, 2, 16, LANES), BF16),
         vm((nb, 16, LANES), F32),
         vm((nb, group, D), BF16),
         vm((length, D), BF16),
@@ -1020,7 +1157,7 @@
         vm((2, length, 2 * LANES), BF16),
         vm((length, part), F32),
         vm((length, part), F32),
-        vm((nb, nb, 8, group), F32),
+        vm((nb, nb, 8, group // 2), F32),
         vm((length, LANES), F32),
         vm((nb, group, part), BF16),
         vm((nb, group, part), BF16),
@@ -1030,29 +1167,26 @@
         vm((nb, group, part), F32),
         vm((length, 4 * part), BF16),
         vm((nb, nb, group, part), BF16),
-        vm((nb, nb, group, part), BF16),
-        vm((nb, nb, 8, group), F32),
+        vm((nb, 2, group, part), BF16),
+        vm((nb, group, part), BF16),
+        vm((nb, group, part), BF16),
+        vm((nb, nb, 8, LANES), F32),
         vm((nb, group, part), BF16),
         vm((nb, group, part), BF16),
         vm((8, LANES), F32),
         vm((8, LANES), F32),
-        vm((nb, nd, rows_table, part), BF16),
-        vm((nz, nb, rows_table, part), BF16),
-        vm((nz, nb, rows_table, part), BF16),
-        vm((nz, nb, rows_table, part), BF16),
-        vm((nb, rows_table, part), F32),
-        vm((nb, rows_table, part), F32),
-        vm((nb, nd, weight_rows, 4 * part), BF16),
-        vm((nz, nb, weight_rows, 4 * part), BF16),
-        vm((nz, nb, weight_rows, 4 * part), BF16),
-        vm((nz, nb, weight_rows, 4 * part), BF16),
-        vm((nb, weight_rows, 4 * part), F32),
-        vm((nb, weight_rows, 4 * part), F32),
-        vm((1, nd, weight_rows, D), BF16),
-        vm((nz, 1, weight_rows, D), BF16),
-        vm((nz, 1, weight_rows, D), BF16),
-        vm((nz, 1, weight_rows, D), BF16),
-        vm((16, LANES), F32), vm((16, LANES), F32), vm((16, LANES), F32), vm((nz, 16, LANES), F32),
+        vm((items, part), F32),
+        vm((2, 2, nz, 2, rows_table, part), BF16),
+        *[vm((nz, 2, 2, rows_table, part), BF16)] * 2,
+        vm((nb, nz, rows_table, part), BF16),
+        vm((2, 2, nz, 2, weight_rows, 4 * part), BF16),
+        *[vm((nz, 2, 2, weight_rows, 4 * part), BF16)] * 2,
+        vm((nb, nz, weight_rows, 4 * part), BF16),
+        vm((nz, 2, weight_rows, D), BF16),
+        *[vm((nz, weight_rows, D), BF16)] * 3,
+        vm((16, LANES), F32),
+        vm((nd, 16, LANES), F32),
+        *[vm((16, LANES), F32)] * 2,
     ]
     whole, far = pl.BlockSpec(memory_space=pltpu.VMEM), pl.BlockSpec(memory_space=pl.ANY)
     between = pl.pallas_call(
@@ -1093,7 +1227,7 @@
     items = item_table.shape[0] * nd
     by_heads = (
         seq_count == 1 and nd % 2 == 0 and D // nb == LANES and group % 256 == 0
-        and items <= 2048 and items // (nb * nd) % 16 == 0 and proj_in.shape[0] % 16 == 0
+        and items == 2048 and proj_in.shape[0] % 16 == 0
         and small_params.shape[1] * nd == LANES and nb == 4 and nd == 8
     )
     if by_heads:

time: 113 us -> 110 us (0.973)
  Pallas kernels: 113 us -> 109 us
    pallas_call x1, Pallas kernels: 110 us -> 106 us  [fused(): pl.pallas_call(functools.partial(fused_kernel, sizes), out_shape=middle,...]
where the time goes in v3:
time: 110 us
  Pallas kernels  109 us (99%)
    pallas_call x1, Pallas kernels, fused(): pl.pallas_call(functools.partial(fused_kernel, sizes), out_shape=middle,...  106 us
    pallas_call x1, Pallas kernels, fused(): pl.pallas_call(functools.partial(finish_kernel, sizes), out_shape=outs, i...  2.97 us

profile of v3, /device:TPU:0, one launch (start us, length us, event | category | flops | bytes accessed | tf_op | source)
XLA Modules:
  0.0 109.7 jit_solution(9412097910653592133)
XLA Ops:
  0.6 106.0 %hstu_step.1 = (bf16[512,512]{1,0:T(8,128)(2,1)}, bf16[4,512,128]{2,1,0:T(8,128)(2,1)}, f32[4,64,128]{2,1,0:T(8,128)}, f32[4,16,512]{2,1,0:T(8,128)}, f32[16,512]{1,0:T(8,128)}, /*index=5*/f32[16,128]{1,0:T(8,128)}) custom-call(s32[1,512]{1,0:T(1,128)} %refs_0_.1, s32[1,512]{1,0:T(1,128)} %refs_1_.1, s32[1,512]{1,0:T(1,128)} %refs_2_.1, ...), custom_call_target="tpu_custom_call" | custom-call | tf_op jit(solution)/shard_map/hstu_step/pallas_call | solution.py:1192
  106.6 3.0 %hstu_finish.1 = (bf16[512,512]{1,0:T(8,128)(2,1)}, f32[512,512]{1,0:T(8,128)}, f32[64,512]{1,0:T(8,128)}, f32[1,64]{1,0:T(1,128)}, f32[1,64]{1,0:T(1,128)}, /*i...) custom-call(bf16[512,512]{1,0:T(8,128)(2,1)} %get-tuple-element.34.r, ...), custom_call_target="tpu_custom_call" | custom-call | tf_op jit(solution)/shard_map/hstu_finish/pallas_call | solution.py:1207

commit v4 on v3

--- a/solution.py
+++ b/solution.py
@@ -468,10 +468,10 @@
         push(own_index, index.at[b], s_index + k, to, s_index + b, away if k == 0 else None)
     for kr, kz in steps:
         w, at_z, to = slab(kr, kz)
-        push(weight_send.at[w], weight.at[y, x, z, core], s_w + kz * nb + kr, to)
+        push(small.at[y, x, z, core], small.at[y, x, z, core], s_s + kz * nb + kr, to)
     for kr, kz in steps:
         w, at_z, to = slab(kr, kz)
-        push(small.at[y, x, z, core], small.at[y, x, z, core], s_s + kz * nb + kr, to)
+        push(weight_send.at[w], weight.at[y, x, z, core], s_w + kz * nb + kr, to)
     s_g = slots(8)
     halves = (slice(0, group // 2), slice(group // 2, group))
     v_x, v_core, v_cross = core * 2 + off_x, other * 2 + x, other * 2 + off_x
@@ -577,14 +577,14 @@
     table_over_z(2)
     for k in range(1, nz):
         push(outw.at[b, d], outw.at[b, d], s_oz + k, z_peer(k))
+    for kz in range(nz):
+        shard_next(1, kz)
     shard_next(0, 0)
     shard_next(0, 1)
     table_over_blk(0)
     table_over_blk(1)
     shard_next(0, 3)
     shard_next(0, 2)
-    for kz in range(nz):
-        shard_next(1, kz)
     cross_over()
     table_over_core(0)
     look_up(near[0], False)
@@ -615,8 +615,8 @@
     masks = (low, lane >= NB)
 
     def embed(t, carry):
-        rows = at(t, step)
-        found = embedded[rows, :] + picked_rows(rows, near[2])
+        rows = at(t, group)
+        found = embedded[rows, :] + picked_rows(rows, near[2], group)
         embedded[rows, :] = found
         found = found.astype(F32)
         mean = jnp.mean(found, axis=1, keepdims=True)
@@ -641,14 +641,14 @@
             key[h, rows, LANES:] = jnp.where(low, time_rows[h], pos_hot).astype(BF16)
         return carry
 
-    lax.fori_loop(0, length // step // 2, embed, 0)
+    lax.fori_loop(0, nb // 2, embed, 0)
     shards_end(2)
     s_oy, s_ox = slots(1), slots(2)
     push(outw.at[b], outw.at[b], s_oy, y_peer)
     for n in range(2):
         arrive(cot_half(v, n), s_g + n, away)
         own_half(n, away)
-    lax.fori_loop(length // step // 2, length // step, embed, 0)
+    lax.fori_loop(nb // 2, nb, embed, 0)
 
     s_st = slots(nb * nb)
     inv_length = 1.0 / length
@@ -769,7 +769,7 @@
                 t = jnp.tanh(x)
                 u = 1.0 + t
                 w = x * u
-                slope = u * (1.0 + x * (1.0 - t))
+                slope = u + w * (1.0 - t)
                 if masked:
                     allowed = iota(w.shape, 0) <= iota(w.shape, 1)
                     w = jnp.where(allowed, w, 0.0)

time: 110 us -> 109 us (level)
  no operation moved by 1% of the time
where the time goes in v4:
time: 109 us
  Pallas kernels  108 us (99%)
    pallas_call x1, Pallas kernels, fused(): pl.pallas_call(functools.partial(fused_kernel, sizes), out_shape=middle,...  105 us
    pallas_call x1, Pallas kernels, fused(): pl.pallas_call(functools.partial(finish_kernel, sizes), out_shape=outs, i...  2.97 us

profile of v4, /device:TPU:0, one launch (start us, length us, event | category | flops | bytes accessed | tf_op | source)
XLA Modules:
  0.0 108.9 jit_solution(1366457869050117460)
XLA Ops:
  0.6 105.1 %hstu_step.1 = (bf16[512,512]{1,0:T(8,128)(2,1)}, bf16[4,512,128]{2,1,0:T(8,128)(2,1)}, f32[4,64,128]{2,1,0:T(8,128)}, f32[4,16,512]{2,1,0:T(8,128)}, f32[16,512]{1,0:T(8,128)}, /*index=5*/f32[16,128]{1,0:T(8,128)}) custom-call(s32[1,512]{1,0:T(1,128)} %refs_0_.1, s32[1,512]{1,0:T(1,128)} %refs_1_.1, s32[1,512]{1,0:T(1,128)} %refs_2_.1, ...), custom_call_target="tpu_custom_call" | custom-call | tf_op jit(solution)/shard_map/hstu_step/pallas_call | solution.py:1192
  105.8 3.0 %hstu_finish.1 = (bf16[512,512]{1,0:T(8,128)(2,1)}, f32[512,512]{1,0:T(8,128)}, f32[64,512]{1,0:T(8,128)}, f32[1,64]{1,0:T(1,128)}, f32[1,64]{1,0:T(1,128)}, /*i...) custom-call(bf16[512,512]{1,0:T(8,128)(2,1)} %get-tuple-element.34.r, ...), custom_call_target="tpu_custom_call" | custom-call | tf_op jit(solution)/shard_map/hstu_finish/pallas_call | solution.py:1207

commit v5 on v4

--- a/solution.py
+++ b/solution.py
@@ -563,12 +563,12 @@
 
     def look_up(at_z, first):
         def body(t, carry):
-            rows = at(t, group)
-            found = picked_rows(rows, at_z, group)
+            rows = at(t, 2 * group)
+            found = picked_rows(rows, at_z, 2 * group)
             embedded[rows, :] = found if first else embedded[rows, :] + found
             return carry
 
-        lax.fori_loop(0, nb, body, 0)
+        lax.fori_loop(0, nb // 2, body, 0)
 
     table_over_z(0)
     table_over_z(1)

time: 109 us -> 109 us (level)
  no operation moved by 1% of the time
where the time goes in v5:
time: 109 us
  Pallas kernels  108 us (99%)
    pallas_call x1, Pallas kernels, fused(): pl.pallas_call(functools.partial(fused_kernel, sizes), out_shape=middle,...  105 us
    pallas_call x1, Pallas kernels, fused(): pl.pallas_call(functools.partial(finish_kernel, sizes), out_shape=outs, i...  2.97 us

profile of v5, /device:TPU:0, one launch (start us, length us, event | category | flops | bytes accessed | tf_op | source)
XLA Modules:
  0.0 108.8 jit_solution(17175455671228341115)
XLA Ops:
  0.6 105.0 %hstu_step.1 = (bf16[512,512]{1,0:T(8,128)(2,1)}, bf16[4,512,128]{2,1,0:T(8,128)(2,1)}, f32[4,64,128]{2,1,0:T(8,128)}, f32[4,16,512]{2,1,0:T(8,128)}, f32[16,512]{1,0:T(8,128)}, /*index=5*/f32[16,128]{1,0:T(8,128)}) custom-call(s32[1,512]{1,0:T(1,128)} %refs_0_.1, s32[1,512]{1,0:T(1,128)} %refs_1_.1, s32[1,512]{1,0:T(1,128)} %refs_2_.1, ...), custom_call_target="tpu_custom_call" | custom-call | tf_op jit(solution)/shard_map/hstu_step/pallas_call | solution.py:1192
  105.7 3.0 %hstu_finish.1 = (bf16[512,512]{1,0:T(8,128)(2,1)}, f32[512,512]{1,0:T(8,128)}, f32[64,512]{1,0:T(8,128)}, f32[1,64]{1,0:T(1,128)}, f32[1,64]{1,0:T(1,128)}, /*i...) custom-call(bf16[512,512]{1,0:T(8,128)(2,1)} %get-tuple-element.34.r, ...), custom_call_target="tpu_custom_call" | custom-call | tf_op jit(solution)/shard_map/hstu_finish/pallas_call | solution.py:1207
